TPU v7x, 32 devices: a whole 2x2x4 slice. The times are simulated.
32 devices in a mesh: orb: 8 (over z, x), slab: 4 (over y, core).
Axes of the slice: x: 2, y: 2, z: 4, core: 2. Of those that a mesh axis runs over, the one named last changes fastest.
Arguments:
- orbitals: bfloat16 [8, 64, 64, 128], P('orb', 'slab'), may hold values from -6 to 6
- pair_table: int32 [64, 3], P('orb'), may hold values from -1 to 7, as said below
Outputs:
- exchange_action: float32 [8, 64, 64, 128], P('orb', 'slab')
Inputs may be any that keep to these rules, and one draw needn't show every extreme that they name: `pair_table`: A live slot holds (m, n, s) with m <= n and s in 0, 1; an empty slot holds -1 in all three columns. A block of 8 slots has its live slots first. No (m, n, s) appears twice in the table. Exactly 36 slots are live, and the 8 blocks hold, in some order, k * 1 live slots for k = 1 to 8.
All inputs are finite; a program needn't handle non-finite values.
Results may differ from a plain program's by a relative error of at most 0.0003.
Values may be sent and summed in bfloat16 or wider, within the bound.
A program may use at most 64 MiB of HBM per device.

v0:
```python
import functools
import math

import jax
import jax.numpy as jnp
import numpy as np
from jax import lax
from jax.experimental import pallas as pl
from jax.experimental.pallas import tpu as pltpu
from jax.sharding import PartitionSpec as P

exchange_fraction = 0.25
cell_ratio = 8.0
MESH = pl.DeviceIdType.MESH
VMEM_SPEC = pl.BlockSpec(memory_space=pltpu.VMEM)
ANY_SPEC = pl.BlockSpec(memory_space=pl.ANY)


def folded(values, grid_len):
    return jnp.minimum(values, grid_len - values).astype(jnp.float32)


def hartley(grid_len):
    rows_idx = np.arange(grid_len)
    angles = 2.0 * math.pi / grid_len * (rows_idx[:, None] * rows_idx[None, :] % grid_len)
    return ((np.cos(angles) + np.sin(angles)) / math.sqrt(grid_len)).astype(np.float32)


def split_const(values):
    high = values.astype(jnp.bfloat16)
    return high, (values - high.astype(np.float32)).astype(jnp.bfloat16)


def split(values):
    high = values.astype(jnp.bfloat16)
    low = (values - high.astype(jnp.float32)).astype(jnp.bfloat16)
    return high, low


def coulomb(grid_len, slab_len, slab_index):
    planes_x = cell_ratio * folded(jnp.arange(grid_len, dtype=jnp.int32), grid_len)
    rows_y = folded(slab_index * slab_len + jnp.arange(slab_len, dtype=jnp.int32), grid_len)
    depth_z = folded(jnp.arange(2 * grid_len, dtype=jnp.int32) % grid_len, grid_len)
    scale_k = 2.0 * math.pi / grid_len * (2.0 * math.pi / grid_len)
    squared = scale_k * (
        planes_x[:, None, None] * planes_x[:, None, None]
        + rows_y[None, :, None] * rows_y[None, :, None]
        + depth_z[None, None, :] * depth_z[None, None, :]
    )
    safe_sq = jnp.where(squared > 0, squared, 1.0)
    return jnp.where(squared > 0, -exchange_fraction / safe_sq, 0.0)


def axis_parts(count):
    inner = 1
    while inner * inner * 4 <= count and count % (inner * 2) == 0:
        inner *= 2
    return count // inner, inner


def peer(index):
    return {"orb": index}


def greet_all(count, me):
    barrier = pltpu.get_barrier_semaphore()
    for step in range(1, count):
        pl.semaphore_signal(
            barrier, inc=1, device_id=peer(lax.rem(me + step, count)), device_id_type=MESH
        )
    pl.semaphore_wait(barrier, count - 1)


def table_kernel(count, table_ref, tables_ref, send_sem, recv_sem):
    me = lax.axis_index("orb")
    greet_all(count, me)

    def tab_copy(step):
        return pltpu.make_async_remote_copy(
            src_ref=table_ref, dst_ref=tables_ref.at[me], send_sem=send_sem.at[step - 1],
            recv_sem=recv_sem.at[step - 1], device_id=peer(lax.rem(me + step, count)),
            device_id_type=MESH)

    for step in range(1, count):
        tab_copy(step).start()
    tables_ref[me] = table_ref[...]
    for step in range(1, count):
        tab_copy(step).wait_recv()
    for step in range(1, count):
        tab_copy(step).wait_send()


def gather_tables(table, count):
    dma = pltpu.SemaphoreType.DMA
    return pl.pallas_call(
        functools.partial(table_kernel, count),
        out_shape=jax.ShapeDtypeStruct((count,) + table.shape, table.dtype),
        in_specs=[VMEM_SPEC],
        out_specs=VMEM_SPEC,
        scratch_shapes=[dma((count - 1,)), dma((count - 1,))],
        compiler_params=pltpu.CompilerParams(collective_id=0, has_side_effects=True),
    )(table)


def depth_turn(rows, depth_ref):
    width = rows.shape[1]
    high, low = split(rows)
    both = jnp.dot(jnp.concatenate([high, low], axis=1), depth_ref[...],
                   preferred_element_type=jnp.float32)
    return both[:, :width] + both[:, width:]


def pair_turn(first, second, left_ref):
    high, low = split(jnp.concatenate([first, second], axis=1))
    return jnp.dot(left_ref[...], jnp.concatenate([high, low, high], axis=0),
                   preferred_element_type=jnp.float32)


def greet_both(n_orb, n_slab, me, me_slab):
    barrier = pltpu.get_barrier_semaphore()
    for step in range(1, n_orb):
        pl.semaphore_signal(barrier, inc=1, device_id=peer(lax.rem(me + step, n_orb)),
                            device_id_type=MESH)
    for step in range(1, n_slab):
        pl.semaphore_signal(barrier, inc=1, device_id={"slab": lax.rem(me_slab + step, n_slab)},
                            device_id_type=MESH)
    pl.semaphore_wait(barrier, n_orb + n_slab - 2)


def chunk_count(slab_len, most):
    return max(1, min(most, slab_len // 2))


def advance_kernel(n_orb, n_slab, chunks, grid_len, ids_ref, own_ref, depth_ref, turn_ref,
                   basis_ref, out_ref, *scratch):
    held = scratch[:chunks]
    (spectra, keep_sem, stay_sem, up_send, up_recv, down_send, down_recv, side_send, side_recv,
     cross_send, cross_recv) = scratch[chunks:]
    outer, inner = axis_parts(n_orb)
    me, me_slab = lax.axis_index("orb"), lax.axis_index("slab")
    z_pos, x_pos = me // inner, me % inner
    couples_own = own_ref.shape[0]
    slots, _, slab_len, width = out_ref.shape
    planes = slab_len // chunks
    rows = planes * grid_len
    greet_both(n_orb, n_slab, me, me_slab)

    def mine(chunk):
        return own_ref.at[:, pl.ds(chunk * rows, rows)]

    def place(chunk, z_at):
        return held[chunk].at[pl.ds((z_at * inner + x_pos) * couples_own, couples_own)]

    def up_copy(chunk, step, src):
        return pltpu.make_async_remote_copy(
            src_ref=src, dst_ref=place(chunk, z_pos - step), send_sem=up_send.at[chunk, step],
            recv_sem=up_recv.at[chunk, step], device_id=peer((z_pos + 1) * inner + x_pos),
            device_id_type=MESH)

    def down_copy(chunk, step, src):
        return pltpu.make_async_remote_copy(
            src_ref=src, dst_ref=place(chunk, z_pos + step), send_sem=down_send.at[chunk, step],
            recv_sem=down_recv.at[chunk, step], device_id=peer((z_pos - 1) * inner + x_pos),
            device_id_type=MESH)

    def side_copy(chunk, hop, z_at, src):
        return pltpu.make_async_remote_copy(
            src_ref=src, dst_ref=place(chunk, z_at), send_sem=side_send.at[chunk, hop - 1, z_at],
            recv_sem=side_recv.at[chunk, hop - 1, z_at],
            device_id=peer(z_pos * inner + lax.rem(x_pos + hop, inner)), device_id_type=MESH)

    def keep_copy(chunk):
        return pltpu.make_async_copy(mine(chunk), place(chunk, z_pos), keep_sem.at[chunk])

    def cross_copy(chunk, hop):
        to = lax.rem(me_slab + hop, n_slab)
        return pltpu.make_async_remote_copy(
            src_ref=spectra.at[chunk, :, :,
                               pl.ds(pl.multiple_of(to * slab_len, slab_len), slab_len)],
            dst_ref=out_ref.at[:, pl.ds(me_slab * slab_len + chunk * planes, planes)],
            send_sem=cross_send.at[chunk, hop - 1], recv_sem=cross_recv.at[chunk, hop - 1],
            device_id={"slab": to}, device_id_type=MESH)

    def stay_copy(chunk):
        return pltpu.make_async_copy(
            spectra.at[chunk, :, :,
                       pl.ds(pl.multiple_of(me_slab * slab_len, slab_len), slab_len)],
            out_ref.at[:, pl.ds(me_slab * slab_len + chunk * planes, planes)],
            stay_sem.at[chunk])

    has_up, has_down = z_pos + 1 < outer, z_pos >= 1

    for chunk in range(chunks):
        @pl.when(has_up)
        def _():
            up_copy(chunk, 0, mine(chunk)).start()

        @pl.when(has_down)
        def _():
            down_copy(chunk, 0, mine(chunk)).start()

        for hop in range(1, inner):
            side_copy(chunk, hop, z_pos, mine(chunk)).start()
        keep_copy(chunk).start()

    def relay(chunk, step):
        @pl.when(z_pos - step >= 0)
        def _():
            got = place(chunk, z_pos - step)
            up_copy(chunk, step - 1, got).wait_recv()

            @pl.when(has_up)
            def _():
                up_copy(chunk, step, got).start()

            for hop in range(1, inner):
                side_copy(chunk, hop, z_pos - step, got).start()

        @pl.when(z_pos + step < outer)
        def _():
            got = place(chunk, z_pos + step)
            down_copy(chunk, step - 1, got).wait_recv()

            @pl.when(has_down)
            def _():
                down_copy(chunk, step, got).start()

            for hop in range(1, inner):
                side_copy(chunk, hop, z_pos + step, got).start()

    def compute(chunk):
        keep_copy(chunk).wait()
        for hop in range(1, inner):
            for z_at in range(outer):
                side_copy(chunk, hop, z_at, mine(chunk)).wait_recv()

        @pl.loop(0, slots)
        def _(slot):
            left = held[chunk][ids_ref[slot, 0]].astype(jnp.float32)
            right = held[chunk][ids_ref[slot, 1]].astype(jnp.float32)
            flipped = ids_ref[slot, 2] == 1
            partner = jnp.where(flipped, pltpu.roll(right, grid_len, 1), right)
            density = jnp.where(ids_ref[slot, 3] == 1, left * partner, 0.0)
            flat = depth_turn(density, depth_ref)
            for x_at in range(0, planes, 2):
                low, mid, high = x_at * grid_len, (x_at + 1) * grid_len, (x_at + 2) * grid_len
                done = pair_turn(flat[low:mid], flat[mid:high], turn_ref)
                spectra[chunk, slot, x_at] = done[:, :width]
                spectra[chunk, slot, x_at + 1] = done[:, width:]

        for hop in range(1, n_slab):
            cross_copy(chunk, hop).start()
        stay_copy(chunk).start()
        basis_ref[:, chunk * rows:(chunk + 1) * rows] = held[chunk][...]

    for wave in range(1, chunks + outer - 1):
        for step in range(outer - 1, 0, -1):
            if 0 <= wave - step < chunks:
                relay(wave - step, step)
        if wave - (outer - 1) >= 0:
            compute(wave - (outer - 1))

    for chunk in range(chunks):
        stay_copy(chunk).wait()
        for hop in range(1, n_slab):
            cross_copy(chunk, hop).wait_recv()
            cross_copy(chunk, hop).wait_send()
        for hop in range(1, inner):
            for z_at in range(outer):
                side_copy(chunk, hop, z_at, mine(chunk)).wait_send()
        for step in range(outer):
            @pl.when(has_up & (z_pos - step >= 0))
            def _():
                up_copy(chunk, step, mine(chunk)).wait_send()

            @pl.when(has_down & (z_pos + step < outer))
            def _():
                down_copy(chunk, step, mine(chunk)).wait_send()


def advance(ids, own, depth_mat, turn_mat, grid_len, n_orb, n_slab):
    outer, inner = axis_parts(n_orb)
    slots = ids.shape[0]
    couples_own, all_rows, width = own.shape
    slab_len = all_rows // grid_len
    chunks = chunk_count(slab_len, 4)
    planes = slab_len // chunks
    rows = planes * grid_len
    sides, slabs = max(inner - 1, 1), max(n_slab - 1, 1)
    dma, vmem, f32 = pltpu.SemaphoreType.DMA, pltpu.VMEM, jnp.float32
    return pl.pallas_call(
        functools.partial(advance_kernel, n_orb, n_slab, chunks, grid_len),
        out_shape=(jax.ShapeDtypeStruct((n_orb * couples_own, all_rows, width), own.dtype),
                   jax.ShapeDtypeStruct((slots, grid_len, slab_len, width), f32)),
        in_specs=[pl.BlockSpec(memory_space=pltpu.SMEM)] + [VMEM_SPEC] * 3,
        out_specs=(VMEM_SPEC, VMEM_SPEC),
        scratch_shapes=[vmem((n_orb * couples_own, rows, width), own.dtype)] * chunks + [
            vmem((chunks, slots, planes, grid_len, width), f32),
            dma((chunks,)), dma((chunks,)),
            dma((chunks, outer)), dma((chunks, outer)), dma((chunks, outer)), dma((chunks, outer)),
            dma((chunks, sides, outer)), dma((chunks, sides, outer)),
            dma((chunks, slabs)), dma((chunks, slabs)),
        ],
        compiler_params=pltpu.CompilerParams(collective_id=2, has_side_effects=True),
    )(ids, own, depth_mat, turn_mat)


def middle_kernel(grid_len, slab_len, in_ref, kernel_ref, turn_ref, out_ref):
    width = in_ref.shape[2]
    for row in range(0, slab_len, 2):
        one = pl.ds(row, grid_len, stride=slab_len)
        two = pl.ds(row + 1, grid_len, stride=slab_len)
        done = pair_turn(in_ref[0, one, :], in_ref[0, two, :], turn_ref)
        back = pair_turn(done[:, :width] * kernel_ref[one, :], done[:, width:] * kernel_ref[two, :],
                         turn_ref)
        out_ref[0, one, :] = back[:, :width]
        out_ref[0, two, :] = back[:, width:]


def return_kernel(n_orb, n_slab, chunks, couples_own, ids_ref, weights_ref, solved_ref, basis_ref,
                  depth_ref, turn_ref, out_ref, back, terms, flat_ref, parts, side_in, line_in, sums,
                  keep_sem, back_send, back_recv, side_send, side_recv, line_send, line_recv):
    outer, inner = axis_parts(n_orb)
    me, me_slab = lax.axis_index("orb"), lax.axis_index("slab")
    z_pos, x_pos = me // inner, me % inner
    slots, grid_len, slab_len, width = solved_ref.shape
    planes = slab_len // chunks
    rows = planes * grid_len

    greet_both(n_orb, n_slab, me, me_slab)
    own_rows = pl.ds(pl.multiple_of(me_slab * slab_len, slab_len), slab_len)

    def back_copy(chunk, hop):
        to = lax.rem(me_slab + hop, n_slab)
        return pltpu.make_async_remote_copy(
            src_ref=solved_ref.at[:, pl.ds(to * slab_len + chunk * planes, planes)],
            dst_ref=back.at[chunk, :, :, own_rows],
            send_sem=back_send.at[chunk, hop - 1], recv_sem=back_recv.at[chunk, hop - 1],
            device_id={"slab": to}, device_id_type=MESH)

    def keep_copy(chunk):
        return pltpu.make_async_copy(
            solved_ref.at[:, pl.ds(me_slab * slab_len + chunk * planes, planes)],
            back.at[chunk, :, :, own_rows], keep_sem.at[chunk])

    def side_copy(chunk, hop, turn):
        z_at = lax.rem(z_pos + turn, outer)
        x_to = lax.rem(x_pos + hop, inner)
        return pltpu.make_async_remote_copy(
            src_ref=parts.at[chunk, z_at * inner + x_to], dst_ref=side_in.at[chunk, hop - 1, turn],
            send_sem=side_send.at[chunk, hop - 1, turn], recv_sem=side_recv.at[chunk, hop - 1, turn],
            device_id=peer(z_pos * inner + x_to), device_id_type=MESH)

    def line_copy(chunk, turn):
        z_at = lax.rem(z_pos + turn, outer)
        return pltpu.make_async_remote_copy(
            src_ref=sums.at[chunk, turn], dst_ref=line_in.at[chunk, turn - 1],
            send_sem=line_send.at[chunk, turn - 1], recv_sem=line_recv.at[chunk, turn - 1],
            device_id=peer(z_at * inner + x_pos), device_id_type=MESH)

    order = list(range(1, outer)) + [0]

    def compute(chunk):
        keep_copy(chunk).wait()
        for hop in range(1, n_slab):
            back_copy(chunk, hop).wait_recv()

        @pl.loop(0, slots)
        def _(slot):
            for x_at in range(0, planes, 2):
                done = pair_turn(back[chunk, slot, x_at], back[chunk, slot, x_at + 1], turn_ref)
                flat_ref[x_at * grid_len:(x_at + 1) * grid_len] = done[:, :width]
                flat_ref[(x_at + 1) * grid_len:(x_at + 2) * grid_len] = done[:, width:]
            potential = depth_turn(flat_ref[...], depth_ref)
            flipped = ids_ref[slot, 2] == 1
            span = pl.ds(chunk * rows, rows)
            right = basis_ref[ids_ref[slot, 1], span].astype(jnp.float32)
            left = basis_ref[ids_ref[slot, 0], span].astype(jnp.float32)
            terms[2 * slot] = potential * jnp.where(flipped, pltpu.roll(right, grid_len, 1), right)
            second = potential * left
            terms[2 * slot + 1] = jnp.where(flipped, pltpu.roll(second, grid_len, 1), second)

        tile = 32

        @pl.loop(0, rows // tile)
        def _(at):
            here = pl.ds(pl.multiple_of(at * tile, tile), tile)

            @pl.loop(0, n_orb)
            def _(owner):
                for k in range(couples_own):
                    total = jnp.zeros((tile, width), jnp.float32)
                    for term in range(2 * slots):
                        total += weights_ref[owner * couples_own + k, term] * terms[term, here]
                    parts[chunk, owner, k, here] = total

        for turn in order:
            for hop in range(1, inner):
                side_copy(chunk, hop, turn).start()

    def forward(chunk):
        for turn in order:
            merged = parts[chunk, lax.rem(z_pos + turn, outer) * inner + x_pos]
            for hop in range(1, inner):
                side_copy(chunk, hop, turn).wait_recv()
                merged = merged + side_in[chunk, hop - 1, turn]
            sums[chunk, turn] = merged
            if turn:
                line_copy(chunk, turn).start()

    for chunk in range(chunks):
        for hop in range(1, n_slab):
            back_copy(chunk, hop).start()
        keep_copy(chunk).start()
    for chunk in range(chunks):
        compute(chunk)
        if chunk:
            forward(chunk - 1)
    forward(chunks - 1)
    for chunk in range(chunks):
        total = sums[chunk, 0]
        for turn in range(1, outer):
            line_copy(chunk, turn).wait_recv()
            total = total + line_in[chunk, turn - 1]
        out_ref[:, chunk * rows:(chunk + 1) * rows] = total
    for chunk in range(chunks):
        for hop in range(1, n_slab):
            back_copy(chunk, hop).wait_send()
        for turn in range(outer):
            for hop in range(1, inner):
                side_copy(chunk, hop, turn).wait_send()
            if turn:
                line_copy(chunk, turn).wait_send()


def return_sum(ids, weights, solved, basis, depth_mat, turn_mat, n_orb, n_slab):
    outer, inner = axis_parts(n_orb)
    slots, grid_len, slab_len, width = solved.shape
    couples_own = basis.shape[0] // n_orb
    chunks = chunk_count(slab_len, 8)
    planes = slab_len // chunks
    rows = planes * grid_len
    sides, lines = max(inner - 1, 1), max(outer - 1, 1)
    dma, vmem, f32 = pltpu.SemaphoreType.DMA, pltpu.VMEM, jnp.float32
    smem = pl.BlockSpec(memory_space=pltpu.SMEM)
    block = (couples_own, rows, width)
    return pl.pallas_call(
        functools.partial(return_kernel, n_orb, n_slab, chunks, couples_own),
        out_shape=jax.ShapeDtypeStruct((couples_own, slab_len * grid_len, width), f32),
        in_specs=[smem, smem] + [VMEM_SPEC] * 4,
        out_specs=VMEM_SPEC,
        scratch_shapes=[
            vmem((chunks, slots, planes, grid_len, width), f32),
            vmem((2 * slots, rows, width), f32),
            vmem((rows, width), f32),
            vmem((chunks, n_orb) + block, f32),
            vmem((chunks, sides, outer) + block, f32),
            vmem((chunks, lines) + block, f32),
            vmem((chunks, outer) + block, f32),
            dma((chunks,)),
            dma((chunks, max(n_slab - 1, 1))), dma((chunks, max(n_slab - 1, 1))),
            dma((chunks, sides, outer)), dma((chunks, sides, outer)),
            dma((chunks, lines)), dma((chunks, lines)),
        ],
        compiler_params=pltpu.CompilerParams(collective_id=1, has_side_effects=True),
    )(ids, weights, solved, basis, depth_mat, turn_mat)


def local(orbitals, pair_table, n_orb, n_slab):
    couples_own, slab_len, grid_len, width = orbitals.shape
    rows = slab_len * grid_len
    capacity = pair_table.shape[0]
    couples = couples_own * n_orb
    padded = jnp.pad(pair_table, ((0, 0), (0, 128 - pair_table.shape[1])), constant_values=-1)
    tables = gather_tables(padded, n_orb)
    table = tables.reshape(n_orb * capacity, 128)[:, :3]

    live_total = sum(capacity * (k + 1) // n_orb for k in range(n_orb))
    per_device = -(-live_total // n_orb)
    is_live = table[:, 0] >= 0
    rank = jnp.cumsum(is_live.astype(jnp.int32)) - 1
    wanted = jnp.arange(per_device, dtype=jnp.int32) * n_orb + lax.axis_index("orb")
    hits = (rank[None, :] == wanted[:, None]) & is_live[None, :]
    picked = jnp.sum(jnp.where(hits[:, :, None], table[None], 0), axis=1)
    used = jnp.any(hits, axis=1).astype(jnp.int32)
    ids = jnp.concatenate([picked, used[:, None]], axis=1)

    mat = hartley(grid_len)
    mat_high, mat_low = split_const(mat)
    turn_mat = jnp.asarray(np.concatenate([mat_high, mat_high, mat_low], axis=1))
    deep_high, deep_low = split_const(np.kron(np.eye(2, dtype=np.float32), mat))
    depth_mat = jnp.asarray(np.block([[deep_high, deep_low],
                                      [deep_high, np.zeros_like(deep_low)]]))
    kernel = coulomb(grid_len, slab_len, lax.axis_index("slab")).reshape(grid_len * slab_len, width)

    def whole(shape):
        return pl.BlockSpec(shape, lambda j, *ids: (0,) * len(shape))

    slot_spec = pl.BlockSpec((1, rows, width), lambda j, *ids: (j, 0, 0))
    slots_shape = jax.ShapeDtypeStruct((per_device, rows, width), jnp.float32)

    gathered, crossed = advance(ids, orbitals.reshape(couples_own, rows, width), depth_mat,
                                turn_mat, grid_len, n_orb, n_slab)
    solved = pl.pallas_call(
        functools.partial(middle_kernel, grid_len, slab_len),
        out_shape=slots_shape,
        grid=(per_device,),
        in_specs=[slot_spec, whole(kernel.shape), whole(turn_mat.shape)],
        out_specs=slot_spec,
    )(crossed.reshape(per_device, rows, width), kernel, turn_mat)
    couple_ids = jnp.arange(couples, dtype=jnp.int32)[:, None]
    first_on = (couple_ids == ids[None, :, 0]) & (ids[None, :, 3] == 1)
    second_on = (couple_ids == ids[None, :, 1]) & (ids[None, :, 3] == 1) & (
        ids[None, :, 0] != ids[None, :, 1])
    weights = jnp.stack([first_on, second_on], axis=2).reshape(couples, 2 * per_device)
    own = return_sum(ids, weights.astype(jnp.float32),
                     solved.reshape(per_device, grid_len, slab_len, width),
                     gathered, depth_mat, turn_mat, n_orb, n_slab)
    own = own.reshape(couples_own, rows, width)
    cell_count = grid_len * grid_len * grid_len

    def swap(values):
        return jnp.concatenate([values[..., grid_len:], values[..., :grid_len]], axis=-1)

    def lanes(values):
        summed = values.reshape(values.shape[:-1] + (2, grid_len)).sum(axis=-1)
        return jnp.repeat(summed, grid_len, axis=-1)

    basis = gathered.astype(jnp.float32)
    turned = swap(own)
    straight = jnp.sum(basis[None] * own[:, None], axis=2)
    across = jnp.sum(basis[None] * turned[:, None], axis=2)
    both = lax.psum(lanes(jnp.stack([straight, across])) / cell_count, "slab")
    kept = jnp.sum(both[0][:, :, None, :] * basis[None], axis=1)
    moved = jnp.sum(both[1][:, :, None, :] * basis[None], axis=1)
    return (own - kept - swap(moved)).reshape(orbitals.shape)


def solution(mesh):
    placed = (P("orb", "slab", None, None), P("orb", None))
    return jax.shard_map(
        functools.partial(local, n_orb=mesh.shape["orb"], n_slab=mesh.shape["slab"]),
        mesh=mesh, in_specs=placed, out_specs=P("orb", "slab", None, None), check_vma=False
    )
```

profile of v0, /device:TPU:0, one launch (start us, length us, event | category | flops | bytes accessed | tf_op | source)
XLA Modules:
  0.0 150.6 jit_solution(18287439544400848642)
XLA Ops:
  0.0 0.8 copy.22
  0.8 0.6 pad.4.table_ref
  1.4 9.7 %shard_map.46 = s32[8,8,128]{2,1,0:T(8,128)} custom-call(s32[8,128]{1,0:T(8,128)} %pad.4.table_ref), custom_call_target="tpu_custom_call" | custom-call | tf_op jit(solution)/shard_map/pallas_call | solution.py:95
  11.1 0.8 copy.31
  12.0 0.8 copy.25
  12.8 0.1 copy.24
  12.9 0.1 reduce-window.8
  13.0 0.1 add_reduce_fusion
  13.1 0.2 fusion.12
  13.3 0.2 select_reduce_fusion
  13.5 0.2 slice_reduce_fusion
  13.7 0.1 compare_and_fusion
  13.8 0.7 copy.27.weights_ref
  14.5 0.1 copy.26
  14.6 0.7 pad_add_fusion.ids_ref
  15.3 0.1 add.78
  15.3 0.1 add.79
  15.4 0.1 add.83
  15.5 1.0 compare_select_fusion.kernel_ref
  16.5 51.9 %shard_map.47 = (bf16[8,1024,128]{2,1,0:T(8,128)(2,1)}, f32[5,64,16,128]{3,2,1,0:T(8,128)}) custom-call(s32[5,4]{1,0:T(8,128)} %pad_add_fusion.ids_ref, bf16[1,1024,128]{2,1,0:T(8,128)(2,1)} %bitcast.33, bf16[256,256]{1,0:T(8,128)(2,1)} %constant.64.clone.depth_ref, bf16[64,192]{1,0:T(8,128)(2,1)} %constant.63.clone.turn_ref), custom_call_target="tpu_custom_call" | custom-call | tf_op jit(solution)/shard_map/pallas_call | solution.py:291
  68.4 6.2 %shard_map.48 = f32[5,1024,128]{2,1,0:T(8,128)} custom-call(f32[5,1024,128]{2,1,0:T(8,128)} %bitcast.30, f32[1024,128]{1,0:T(8,128)} %compare_select_fusion.kernel_ref, bf16[64,192]{1,0:T(8,128)(2,1)} %constant.63.clone.turn_ref), custom_call_target="tpu_custom_call" | custom-call | tf_op jit(solution)/shard_map/pallas_call | solution.py:504
  74.6 64.2 %shard_map.49 = f32[1,1024,128]{2,1,0:T(8,128)} custom-call(s32[5,4]{1,0:T(8,128)} %pad_add_fusion.ids_ref, f32[8,10]{1,0:T(8,128)} %copy.27.weights_ref, f32[5,64,16,128]{3,2,1,0:T(8,128)} %bitcast.28, bf16[8,1024,128]{2,1,0:T(8,128)(2,1)} %get-tuple-element.8.basis_ref, bf16[256,256]{1,0:T(8,128)(2,1)} %constant.64.clone.depth_ref, ...), custom_call_target="tpu_custom_call" | custom-call | tf_op jit(solution)/shard_map/pallas_call | solution.py:447
  138.9 0.0 copy-start
  138.9 0.0 copy-start.1
  138.9 1.6 %fusion.14 = (f32[1,1024,64]{2,1,0:T(8,128)S(1)}, f32[1,1024,64]{2,1,0:T(8,128)S(1)}) fusion(f32[1,1024,128]{2,1,0:T(8,128)} %shard_map.49), kind=kLoop, calls=%fused_computation.45 | loop fusion | bytes 1048576 | tf_op jit(solution)/shard_map/slice | solution.py:523
  140.4 0.2 maximum_bitcast_fusion
  140.6 0.1 copy-done
  140.8 0.1 copy-done.1
  140.8 0.7 fusion
  141.6 0.1 stack.15
  141.6 0.1 stack.16
  141.7 0.1 maximum_reduce_fusion
  141.8 0.1 broadcast_in_dim.31
  141.9 0.1 div.19
  142.0 6.6 %psum.7 = f32[2,1,8,128]{3,2,1,0:T(8,128)S(1)} all-reduce(f32[2,1,8,128]{3,2,1,0:T(8,128)S(1)} %div.19), channel_id=1, replica_groups=mesh['orb'=8,'slab'=4] {'slab'}, use_global_device_ids=true, to_apply=%region_6.7 | all-reduce | flops 2048 | bytes 16384 | tf_op jit(solution)/shard_map/psum | solution.py:533
  148.6 0.7 fusion.2
  149.4 0.2 fusion.13
  149.6 1.0 maximum_subtract_fusion
  (13 shorter events, 0.1 us)
Async XLA Ops:
  138.9 1.9 %copy-start = (bf16[8,1024,128]{2,1,0:T(8,128)(2,1)S(1)}, bf16[8,1024,128]{2,1,0:T(8,128)(2,1)}, u32[]{:S(2)}) copy-start(bf16[8,1024,128]{2,1,0:T(8,128)(2,1)} %get-tuple-element.8.basis_ref) | copy-start | bytes 6291460
  138.9 2.0 %copy-start.1 = (f32[1,1024,128]{2,1,0:T(8,128)S(1)}, f32[1,1024,128]{2,1,0:T(8,128)}, u32[]{:S(2)}) copy-start(f32[1,1024,128]{2,1,0:T(8,128)} %shard_map.49) | copy-start | bytes 1572868
where the time goes:
time: 151 us
  Pallas kernels  132 us (87%)
  blocking collectives  6.61 us (4%)
  local copies, waits for them, and re-layouts  6.58 us (4%)
  other arithmetic  5.19 us (3%)
    pallas_call x1, Pallas kernels, return_sum(): pl.pallas_call(functools.partial(return_kernel, n_orb, n_slab, chunks, co...  64.2 us
    pallas_call x1, Pallas kernels, advance(): pl.pallas_call(functools.partial(advance_kernel, n_orb, n_slab, chunks, g...  51.9 us
    pallas_call x1, Pallas kernels, gather_tables(): pl.pallas_call(functools.partial(table_kernel, count), out_shape=jax.Shap...  9.73 us
    psum x1, blocking collectives, local(): both = lax.psum(lanes(jnp.stack([straight, across])) / cell_count, 'slab')  6.61 us
    pallas_call x1, Pallas kernels, local(): pl.pallas_call(functools.partial(middle_kernel, grid_len, slab_len), out_...  6.24 us

commit v1 on v0

--- a/solution.py
+++ b/solution.py
@@ -478,7 +478,9 @@
     live_total = sum(capacity * (k + 1) // n_orb for k in range(n_orb))
     per_device = -(-live_total // n_orb)
     is_live = table[:, 0] >= 0
-    rank = jnp.cumsum(is_live.astype(jnp.int32)) - 1
+    places = jnp.arange(n_orb * capacity, dtype=jnp.int32)
+    ahead = (places[None, :] < places[:, None]) & is_live[None, :]
+    rank = jnp.sum(ahead.astype(jnp.int32), axis=1)
     wanted = jnp.arange(per_device, dtype=jnp.int32) * n_orb + lax.axis_index("orb")
     hits = (rank[None, :] == wanted[:, None]) & is_live[None, :]
     picked = jnp.sum(jnp.where(hits[:, :, None], table[None], 0), axis=1)

time: 151 us -> 151 us (level)
  no operation moved by 1% of the time
where the time goes in v1:
time: 151 us; the launch traced here: 150 us
  Pallas kernels  132 us (87%)
  blocking collectives  6.59 us (4%)
  other arithmetic  5.86 us (4%)
  local copies, waits for them, and re-layouts  5.74 us (4%)
    pallas_call x1, Pallas kernels, return_sum(): pl.pallas_call(functools.partial(return_kernel, n_orb, n_slab, chunks, co...  64.2 us
    pallas_call x1, Pallas kernels, advance(): pl.pallas_call(functools.partial(advance_kernel, n_orb, n_slab, chunks, g...  51.9 us
    pallas_call x1, Pallas kernels, gather_tables(): pl.pallas_call(functools.partial(table_kernel, count), out_shape=jax.Shap...  9.73 us
    psum x1, blocking collectives, local(): both = lax.psum(lanes(jnp.stack([straight, across])) / cell_count, 'slab')  6.59 us
    pallas_call x1, Pallas kernels, local(): pl.pallas_call(functools.partial(middle_kernel, grid_len, slab_len), out_...  6.24 us

profile of v1, /device:TPU:0, one launch (start us, length us, event | category | flops | bytes accessed | tf_op | source)
XLA Modules:
  0.0 150.4 jit_solution(14211080471827097185)
XLA Ops:
  0.0 0.8 copy.19
  0.8 0.6 pad.4.table_ref
  1.4 9.7 %shard_map.46 = s32[8,8,128]{2,1,0:T(8,128)} custom-call(s32[8,128]{1,0:T(8,128)} %pad.4.table_ref), custom_call_target="tpu_custom_call" | custom-call | tf_op jit(solution)/shard_map/pallas_call | solution.py:95
  11.1 0.8 copy.21
  12.0 0.8 slice_compare_fusion
  12.7 0.1 copy.28
  12.8 0.1 convert_reduce_fusion
  12.9 0.2 fusion.13
  13.1 0.2 select_reduce_fusion
  13.3 0.2 slice_reduce_fusion
  13.5 0.1 compare_and_fusion
  13.7 0.7 copy.23.weights_ref
  14.3 0.1 copy.22
  14.4 0.7 pad_add_fusion.ids_ref
  15.1 0.1 add.72
  15.2 0.1 add.73
  15.2 0.1 add.77
  15.3 1.0 compare_select_fusion.kernel_ref
  16.3 51.9 %shard_map.47 = (bf16[8,1024,128]{2,1,0:T(8,128)(2,1)}, f32[5,64,16,128]{3,2,1,0:T(8,128)}) custom-call(s32[5,4]{1,0:T(8,128)} %pad_add_fusion.ids_ref, bf16[1,1024,128]{2,1,0:T(8,128)(2,1)} %bitcast.31, bf16[256,256]{1,0:T(8,128)(2,1)} %constant.59.clone.depth_ref, bf16[64,192]{1,0:T(8,128)(2,1)} %constant.58.clone.turn_ref), custom_call_target="tpu_custom_call" | custom-call | tf_op jit(solution)/shard_map/pallas_call | solution.py:291
  68.2 6.2 %shard_map.48 = f32[5,1024,128]{2,1,0:T(8,128)} custom-call(f32[5,1024,128]{2,1,0:T(8,128)} %bitcast.28, f32[1024,128]{1,0:T(8,128)} %compare_select_fusion.kernel_ref, bf16[64,192]{1,0:T(8,128)(2,1)} %constant.58.clone.turn_ref), custom_call_target="tpu_custom_call" | custom-call | tf_op jit(solution)/shard_map/pallas_call | solution.py:506
  74.4 64.2 %shard_map.49 = f32[1,1024,128]{2,1,0:T(8,128)} custom-call(s32[5,4]{1,0:T(8,128)} %pad_add_fusion.ids_ref, f32[8,10]{1,0:T(8,128)} %copy.23.weights_ref, f32[5,64,16,128]{3,2,1,0:T(8,128)} %bitcast.26, bf16[8,1024,128]{2,1,0:T(8,128)(2,1)} %get-tuple-element.8.basis_ref, bf16[256,256]{1,0:T(8,128)(2,1)} %constant.59.clone.depth_ref, ...), custom_call_target="tpu_custom_call" | custom-call | tf_op jit(solution)/shard_map/pallas_call | solution.py:447
  138.7 0.0 copy-start
  138.7 0.0 copy-start.1
  138.7 1.6 %fusion.15 = (f32[1,1024,64]{2,1,0:T(8,128)S(1)}, f32[1,1024,64]{2,1,0:T(8,128)S(1)}) fusion(f32[1,1024,128]{2,1,0:T(8,128)} %shard_map.49), kind=kLoop, calls=%fused_computation.46 | loop fusion | bytes 1048576 | tf_op jit(solution)/shard_map/slice | solution.py:525
  140.3 0.2 maximum_bitcast_fusion
  140.5 0.1 copy-done
  140.6 0.1 copy-done.1
  140.7 0.7 fusion
  141.4 0.1 stack.15
  141.5 0.1 stack.16
  141.5 0.1 maximum_reduce_fusion
  141.7 0.1 broadcast_in_dim.31
  141.7 0.1 div.19
  141.8 6.6 %psum.7 = f32[2,1,8,128]{3,2,1,0:T(8,128)S(1)} all-reduce(f32[2,1,8,128]{3,2,1,0:T(8,128)S(1)} %div.19), channel_id=1, replica_groups=mesh['orb'=8,'slab'=4] {'slab'}, use_global_device_ids=true, to_apply=%region_6.7 | all-reduce | flops 2048 | bytes 16384 | tf_op jit(solution)/shard_map/psum | solution.py:535
  148.4 0.7 fusion.2
  149.2 0.2 fusion.14
  149.4 1.0 maximum_subtract_fusion
  (12 shorter events, 0.1 us)
Async XLA Ops:
  138.7 1.9 %copy-start = (bf16[8,1024,128]{2,1,0:T(8,128)(2,1)S(1)}, bf16[8,1024,128]{2,1,0:T(8,128)(2,1)}, u32[]{:S(2)}) copy-start(bf16[8,1024,128]{2,1,0:T(8,128)(2,1)} %get-tuple-element.8.basis_ref) | copy-start | bytes 6291460
  138.7 2.0 %copy-start.1 = (f32[1,1024,128]{2,1,0:T(8,128)S(1)}, f32[1,1024,128]{2,1,0:T(8,128)}, u32[]{:S(2)}) copy-start(f32[1,1024,128]{2,1,0:T(8,128)} %shard_map.49) | copy-start | bytes 1572868

commit v2 on v0

v2 whole, which is shorter than its diff:
```python
import functools
import math

import jax
import jax.numpy as jnp
import numpy as np
from jax import lax
from jax.experimental import pallas as pl
from jax.experimental.pallas import tpu as pltpu
from jax.sharding import PartitionSpec as P

exchange_fraction = 0.25
cell_ratio = 8.0
lines_own = 8
code_peak = 32760.0
MESH = pl.DeviceIdType.MESH
VMEM_SPEC = pl.BlockSpec(memory_space=pltpu.VMEM)
f32 = jnp.float32


def hartley(grid_len):
    rows_idx = np.arange(grid_len)
    angles = 2.0 * math.pi / grid_len * (rows_idx[:, None] * rows_idx[None, :] % grid_len)
    return ((np.cos(angles) + np.sin(angles)) / math.sqrt(grid_len)).astype(np.float32)


def split_const(values):
    high = values.astype(jnp.bfloat16)
    return high, (values - high.astype(np.float32)).astype(jnp.bfloat16)


def split(values):
    high = values.astype(jnp.bfloat16)
    low = (values - high.astype(f32)).astype(jnp.bfloat16)
    return high, low


def depth_turn(rows, depth_ref):
    width = rows.shape[1]
    high, low = split(rows)
    both = jnp.dot(jnp.concatenate([high, low], axis=1), depth_ref[...],
                   preferred_element_type=f32)
    return both[:, :width] + both[:, width:]


def pair_turn(first, second, left_ref):
    high, low = split(jnp.concatenate([first, second], axis=1))
    return jnp.dot(left_ref[...], jnp.concatenate([high, low, high], axis=0),
                   preferred_element_type=f32)


def encode(block):
    peak = jnp.max(jnp.abs(block), axis=0, keepdims=True)
    inverse = jnp.where(peak > 1e-34, code_peak / jnp.maximum(peak, 1e-34), 0.0)
    return jnp.round(block * inverse).astype(jnp.int32).astype(jnp.int16), peak * (1.0 / code_peak)


def decode(code, unit):
    return code.astype(jnp.int32).astype(f32) * unit


def remote(src, dst, send_sem, recv_sem, device):
    return pltpu.make_async_remote_copy(src_ref=src, dst_ref=dst, send_sem=send_sem, recv_sem=recv_sem,
                                        device_id=device, device_id_type=MESH)


def action_kernel(n_orb, n_slab, half, slots, chunks, grid_len, table_ref, own_ref, depth_ref,
                  turn_ref, out_ref, *scratch):
    held = scratch[:chunks]
    (tab_own, tables, tab_s, starts, ids, chosen, gain, kern, fsend, funit, frecv, frunit, work, turned,
     bsend, bunit, brecv, brunit, terms, parts, rsend, runit, rrecv, rrunit, sums, overlap, overlap_in,
     coef, ysend,
     tab_sem, tab_send, tab_recv, own_sem, g_send, g_recv, stay_sem, f_send, f_recv, keep_sem, b_send,
     b_recv, r_send, r_recv, p_send, p_recv, y_send, y_recv) = scratch[chunks:]
    me, me_slab = lax.axis_index("orb"), lax.axis_index("slab")
    group, part = me // half, me % half
    groups, members = n_orb // half, n_slab * half
    place = me_slab * half + part
    own_couples, _, width = own_ref.shape
    couples = n_orb * own_couples
    shared = half * own_couples
    capacity = table_ref.shape[1]
    lines = grid_len // members
    planes = grid_len // members // chunks
    rows = planes * grid_len
    tile = planes * lines

    def line_peer(step):
        return {"orb": lax.rem(me + step, n_orb)}

    def member(step):
        to = lax.rem(place + step, members)
        return to, {"orb": group * half + to % half, "slab": to // half}

    barrier = pltpu.get_barrier_semaphore()
    for step in range(1, n_orb):
        pl.semaphore_signal(barrier, inc=1, device_id=line_peer(step), device_id_type=MESH)
    for slab_step in range(1, n_slab):
        for other in range(half):
            pl.semaphore_signal(
                barrier, inc=1, device_id={"orb": group * half + other,
                                           "slab": lax.rem(me_slab + slab_step, n_slab)},
                device_id_type=MESH)
    pl.semaphore_wait(barrier, n_orb - 1 + (n_slab - 1) * half)

    def plane_rows(which, chunk):
        return pl.ds(pl.multiple_of((which * chunks + chunk) * rows, rows), rows)

    def tab_copy(step):
        return remote(tab_own, tables.at[me], tab_send.at[step - 1], tab_recv.at[step - 1],
                      line_peer(step))

    def gather_copy(chunk, step):
        to = lax.rem(me + step, n_orb)
        return remote(own_ref.at[:, plane_rows(to % half, chunk)],
                      held[chunk].at[pl.ds(me * own_couples, own_couples)],
                      g_send.at[chunk, step - 1], g_recv.at[chunk, step - 1], line_peer(step))

    def own_copy(chunk):
        return pltpu.make_async_copy(own_ref.at[:, plane_rows(part, chunk)],
                                     held[chunk].at[pl.ds(me * own_couples, own_couples)],
                                     own_sem.at[chunk])

    def fwd_copies(chunk, step):
        to, device = member(step)
        return (remote(fsend.at[chunk, to], frecv.at[:, place, chunk], f_send.at[0, chunk, step - 1],
                       f_recv.at[0, chunk, step - 1], device),
                remote(funit.at[chunk, to], frunit.at[place, chunk], f_send.at[1, chunk, step - 1],
                       f_recv.at[1, chunk, step - 1], device))

    def fwd_stay(chunk):
        return (pltpu.make_async_copy(fsend.at[chunk, place], frecv.at[:, place, chunk],
                                      stay_sem.at[0, chunk]),
                pltpu.make_async_copy(funit.at[chunk, place], frunit.at[place, chunk],
                                      stay_sem.at[1, chunk]))

    def back_copies(chunk, step):
        to, device = member(step)
        return (remote(bsend.at[chunk, to], brecv.at[chunk, place], b_send.at[0, chunk, step - 1],
                       b_recv.at[0, chunk, step - 1], device),
                remote(bunit.at[chunk, to], brunit.at[chunk, place], b_send.at[1, chunk, step - 1],
                       b_recv.at[1, chunk, step - 1], device))

    def back_stay(chunk):
        return (pltpu.make_async_copy(bsend.at[chunk, place], brecv.at[chunk, place],
                                      keep_sem.at[0, chunk]),
                pltpu.make_async_copy(bunit.at[chunk, place], brunit.at[chunk, place],
                                      keep_sem.at[1, chunk]))

    def sum_copies(chunk, step):
        to = lax.rem(group + step, groups)
        theirs = pl.ds(to * shared, shared)
        device = {"orb": to * half + part}
        return (remote(rsend.at[chunk, theirs], rrecv.at[chunk, step - 1], r_send.at[0, chunk, step - 1],
                       r_recv.at[0, chunk, step - 1], device),
                remote(runit.at[chunk, theirs], rrunit.at[chunk, step - 1], r_send.at[1, chunk, step - 1],
                       r_recv.at[1, chunk, step - 1], device))

    def overlap_copy(step):
        return remote(overlap, overlap_in.at[step - 1], p_send.at[step - 1], p_recv.at[step - 1],
                      member(step)[1])

    def result_copy(chunk, hop):
        to = lax.rem(part + hop, half)
        return remote(ysend.at[chunk, pl.ds(to * own_couples, own_couples)],
                      out_ref.at[:, plane_rows(part, chunk)], y_send.at[chunk, hop - 1],
                      y_recv.at[chunk, hop - 1], {"orb": group * half + to})

    tab_own[...] = jnp.full(tab_own.shape, -1, jnp.int32)
    tab_own[0:3, 0:capacity] = table_ref[...]
    for step in range(1, n_orb):
        tab_copy(step).start()
    for chunk in range(chunks):
        for step in range(1, n_orb):
            gather_copy(chunk, step).start()
        own_copy(chunk).start()
    tables[me] = tab_own[...]

    kz = lax.broadcasted_iota(jnp.int32, (grid_len, width), 1) % grid_len
    fz = jnp.minimum(kz, grid_len - kz).astype(f32)
    ky = lax.broadcasted_iota(jnp.int32, (grid_len, width), 0)
    fy = jnp.minimum(ky, grid_len - ky).astype(f32)
    plane_sq = fy * fy + fz * fz
    deep = cell_ratio * cell_ratio
    gain[...] = 1.0 / jnp.where(plane_sq > 0, plane_sq, deep)
    fx = cell_ratio * fy
    scale_k = (2.0 * math.pi / grid_len) * (2.0 * math.pi / grid_len)
    for line in range(lines):
        at = place * lines + line
        fl = jnp.minimum(at, grid_len - at).astype(f32)
        plane = fl * fl + fz * fz
        whole = fx * fx + plane
        level = jnp.where(plane > 0, plane, deep)
        kern[line * grid_len:(line + 1) * grid_len] = jnp.where(
            whole > 0, (-exchange_fraction / scale_k) * level / jnp.where(whole > 0, whole, 1.0), 0.0)
    terms[2 * slots] = jnp.zeros(terms.shape[1:], f32)
    overlap[...] = jnp.zeros(overlap.shape, f32)
    for chunk in range(chunks):
        for ref in (funit, bunit):
            ref[chunk] = jnp.zeros(ref.shape[1:], f32)

    for step in range(1, n_orb):
        tab_copy(step).wait_recv()
    to_scalars = pltpu.make_async_copy(tables, tab_s, tab_sem)
    to_scalars.start()
    to_scalars.wait()

    def count_block(block, total):
        starts[block] = total
        return lax.fori_loop(
            0, capacity, lambda k, sum_in: sum_in + (tab_s[block, 0, k] >= 0).astype(jnp.int32), total)

    live = lax.fori_loop(0, n_orb, count_block, jnp.int32(0))

    @pl.loop(0, slots)
    def _(slot):
        wanted = slot * groups + group
        used = wanted < live
        block = lax.fori_loop(
            1, n_orb, lambda b, sum_in: sum_in + (starts[b] <= wanted).astype(jnp.int32), jnp.int32(0))
        column = jnp.clip(wanted - starts[block], 0, capacity - 1)
        for k in range(3):
            ids[slot, k] = jnp.maximum(tab_s[block, k, column], 0)
        first = jnp.where(used, tab_s[block, 0, column], -1)
        second = jnp.where(used, tab_s[block, 1, column], -1)

        @pl.loop(0, couples)
        def _(couple):
            chosen[couple, slot] = jnp.where(
                first == couple, 2 * slot, jnp.where(second == couple, 2 * slot + 1, 2 * slots))

    def pair_of(chunk, slot):
        left = held[chunk][ids[slot, 0]].astype(f32)
        right = held[chunk][ids[slot, 1]].astype(f32)
        flipped = ids[slot, 2] == 1
        return left, jnp.where(flipped, pltpu.roll(right, grid_len, 1), right), flipped

    def advance(chunk):
        own_copy(chunk).wait()
        for step in range(1, n_orb):
            gather_copy(chunk, step).wait_recv()

        @pl.loop(0, slots)
        def _(slot):
            left, partner, _ = pair_of(chunk, slot)
            flat = depth_turn(left * partner, depth_ref)
            done = pair_turn(flat[:grid_len], flat[grid_len:], turn_ref)
            one, two = done[:, :width] * gain[...], done[:, width:] * gain[...]
            for to in range(members):
                span = slice(to * lines, (to + 1) * lines)
                code, unit = encode(jnp.concatenate([one[span], two[span]], axis=0))
                fsend[chunk, to, slot] = code
                funit[chunk, to, pl.ds(slot, 1)] = unit

        for step in range(1, members):
            for copy in fwd_copies(chunk, step):
                copy.start()
        for copy in fwd_stay(chunk):
            copy.start()

    for chunk in range(chunks):
        advance(chunk)

    for chunk in range(chunks):
        for copy in fwd_stay(chunk):
            copy.wait()
        for step in range(1, members):
            for copy in fwd_copies(chunk, step):
                copy.wait_recv()

    @pl.loop(0, slots)
    def _(slot):
        for src in range(members):
            for chunk in range(chunks):
                at = (src * chunks + chunk) * tile
                work[at:at + tile] = decode(frecv[slot, src, chunk], frunit[src, chunk, pl.ds(slot, 1)])
        for line in range(0, lines, 2):
            one, two = pl.ds(line, grid_len, stride=lines), pl.ds(line + 1, grid_len, stride=lines)
            low, mid, high = line * grid_len, (line + 1) * grid_len, (line + 2) * grid_len
            done = pair_turn(work[one, :], work[two, :], turn_ref)
            back = pair_turn(done[:, :width] * kern[low:mid], done[:, width:] * kern[mid:high], turn_ref)
            turned[one, :] = back[:, :width]
            turned[two, :] = back[:, width:]
        for to in range(members):
            for chunk in range(chunks):
                at = (to * chunks + chunk) * tile
                code, unit = encode(turned[at:at + tile])
                bsend[chunk, to, slot] = code
                bunit[chunk, to, pl.ds(slot, 1)] = unit

    for chunk in range(chunks):
        for step in range(1, members):
            for copy in back_copies(chunk, step):
                copy.start()
        for copy in back_stay(chunk):
            copy.start()

    def retreat(chunk):
        for copy in back_stay(chunk):
            copy.wait()
        for step in range(1, members):
            for copy in back_copies(chunk, step):
                copy.wait_recv()

        @pl.loop(0, slots)
        def _(slot):
            blocks = [decode(brecv[chunk, src, slot], brunit[chunk, src, pl.ds(slot, 1)])
                      for src in range(members)]
            done = pair_turn(jnp.concatenate([block[:lines] for block in blocks], axis=0),
                             jnp.concatenate([block[lines:] for block in blocks], axis=0), turn_ref)
            potential = depth_turn(jnp.concatenate([done[:, :width], done[:, width:]], axis=0), depth_ref)
            left, partner, flipped = pair_of(chunk, slot)
            terms[2 * slot] = potential * partner
            second = potential * left
            terms[2 * slot + 1] = jnp.where(flipped, pltpu.roll(second, grid_len, 1), second)

        @pl.loop(0, couples)
        def _(couple):
            total = terms[chosen[couple, 0]]
            for slot in range(1, slots):
                total = total + terms[chosen[couple, slot]]
            parts[chunk, couple] = total
            code, unit = encode(total)
            rsend[chunk, couple] = code
            runit[chunk, couple] = jnp.broadcast_to(unit, runit.shape[2:])

        for step in range(1, groups):
            for copy in sum_copies(chunk, step):
                copy.start()

    def collect(chunk):
        for step in range(1, groups):
            for copy in sum_copies(chunk, step):
                copy.wait_recv()
        for k in range(shared):
            total = parts[chunk, group * shared + k]
            for step in range(1, groups):
                total = total + decode(rrecv[chunk, step - 1, k], rrunit[chunk, step - 1, k, 0:1])
            sums[chunk, k] = total
            across = pltpu.roll(total, grid_len, 1)

            @pl.loop(0, couples)
            def _(couple):
                basis = held[chunk][couple].astype(f32)
                for kind, field in enumerate((total, across)):
                    at = pl.ds((kind * shared + k) * couples + couple, 1)
                    overlap[at] += jnp.sum(basis * field, axis=0, keepdims=True)

    for chunk in range(chunks):
        retreat(chunk)
        if chunk:
            collect(chunk - 1)
    collect(chunks - 1)

    for step in range(1, members):
        overlap_copy(step).start()
    total = overlap[...]
    for step in range(1, members):
        overlap_copy(step).wait_recv()
        total = total + overlap_in[step - 1]
    total = total * (1.0 / (grid_len * grid_len * grid_len))
    lane = lax.broadcasted_iota(jnp.int32, total.shape, 1)
    lower = jnp.sum(jnp.where(lane < grid_len, total, 0.0), axis=1, keepdims=True)
    upper = jnp.sum(jnp.where(lane < grid_len, 0.0, total), axis=1, keepdims=True)
    coef[...] = jnp.where(lane < grid_len, lower, upper)

    strip = rows // 4
    for chunk in range(chunks):
        @pl.loop(0, rows // strip)
        def _(at):
            here = pl.ds(pl.multiple_of(at * strip, strip), strip)
            kept = [jnp.zeros((strip, width), f32) for _ in range(2 * shared)]
            for couple in range(couples):
                basis = held[chunk][couple, here].astype(f32)
                for k in range(2 * shared):
                    row = k * couples + couple
                    kept[k] = kept[k] + coef[row:row + 1] * basis
            for k in range(shared):
                ysend[chunk, k, here] = (sums[chunk, k, here] - kept[k]
                                         - pltpu.roll(kept[shared + k], grid_len, 1))

        for hop in range(1, half):
            result_copy(chunk, hop).start()
        out_ref[:, plane_rows(part, chunk)] = ysend[chunk, pl.ds(part * own_couples, own_couples)]

    for chunk in range(chunks):
        for hop in range(1, half):
            result_copy(chunk, hop).wait()
        for step in range(1, members):
            for copy in fwd_copies(chunk, step) + back_copies(chunk, step):
                copy.wait_send()
        for step in range(1, groups):
            for copy in sum_copies(chunk, step):
                copy.wait_send()
        for step in range(1, n_orb):
            gather_copy(chunk, step).wait_send()
    for step in range(1, members):
        overlap_copy(step).wait_send()
    for step in range(1, n_orb):
        tab_copy(step).wait_send()


def local(orbitals, pair_table, n_orb, n_slab):
    own_couples, slab_len, grid_len, width = orbitals.shape
    capacity = pair_table.shape[0]
    half = max(1, grid_len // (lines_own * n_slab))
    members = n_slab * half
    groups = n_orb // half
    live_total = sum(capacity * (k + 1) // n_orb for k in range(n_orb))
    slots = -(-live_total // groups)
    couples, shared = n_orb * own_couples, half * own_couples
    lines = grid_len // members
    chunks = lines // 2
    rows, tile = 2 * grid_len, 2 * lines
    slots_pad = -(-slots // 8) * 8
    tab_lanes = -(-capacity // 128) * 128

    mat = hartley(grid_len)
    mat_high, mat_low = split_const(mat)
    turn_mat = jnp.asarray(np.concatenate([mat_high, mat_high, mat_low], axis=1))
    deep_high, deep_low = split_const(np.kron(np.eye(2, dtype=np.float32), mat))
    depth_mat = jnp.asarray(np.block([[deep_high, deep_low], [deep_high, np.zeros_like(deep_low)]]))

    dma, vmem, smem = pltpu.SemaphoreType.DMA, pltpu.VMEM, pltpu.SMEM
    i32, i16 = jnp.int32, jnp.int16
    coded = vmem((chunks, members, slots, tile, width), i16)
    units = vmem((chunks, members, slots_pad, width), f32)
    lines_sem = dma((chunks, n_orb - 1))
    cross_sem = dma((2, chunks, members - 1))
    steps = max(groups - 1, 1)
    sum_sem = dma((2, chunks, steps))
    hops = max(half - 1, 1)
    out = pl.pallas_call(
        functools.partial(action_kernel, n_orb, n_slab, half, slots, chunks, grid_len),
        out_shape=jax.ShapeDtypeStruct((own_couples, slab_len * grid_len, width), f32),
        in_specs=[VMEM_SPEC] * 4,
        out_specs=VMEM_SPEC,
        scratch_shapes=[vmem((couples, rows, width), orbitals.dtype)] * chunks + [
            vmem((8, tab_lanes), i32), vmem((n_orb, 8, tab_lanes), i32), smem((n_orb, 8, tab_lanes), i32),
            smem((n_orb,), i32), smem((slots, 3), i32), smem((couples, slots), i32),
            vmem((grid_len, width), f32), vmem((lines * grid_len, width), f32),
            coded, units,
            vmem((slots, members, chunks, tile, width), i16), vmem((members, chunks, slots_pad, width), f32),
            vmem((lines * grid_len, width), f32), vmem((lines * grid_len, width), f32),
            coded, units, coded, units,
            vmem((2 * slots + 1, rows, width), f32),
            vmem((chunks, couples, rows, width), f32),
            vmem((chunks, couples, rows, width), i16), vmem((chunks, couples, 8, width), f32),
            vmem((chunks, steps, shared, rows, width), i16), vmem((chunks, steps, shared, 8, width), f32),
            vmem((chunks, shared, rows, width), f32),
            vmem((2 * shared * couples, width), f32),
            vmem((members - 1, 2 * shared * couples, width), f32),
            vmem((2 * shared * couples, width), f32),
            vmem((chunks, shared, rows, width), f32),
            dma, dma((n_orb - 1,)), dma((n_orb - 1,)), dma((chunks,)), lines_sem, lines_sem,
            dma((2, chunks)), cross_sem, cross_sem, dma((2, chunks)), cross_sem, cross_sem,
            sum_sem, sum_sem, dma((members - 1,)), dma((members - 1,)),
            dma((chunks, hops)), dma((chunks, hops)),
        ],
        compiler_params=pltpu.CompilerParams(collective_id=0, has_side_effects=True,
                                             vmem_limit_bytes=56 << 20),
    )(pair_table.T, orbitals.reshape(own_couples, slab_len * grid_len, width), depth_mat, turn_mat)
    return out.reshape(orbitals.shape)


def solution(mesh):
    placed = (P("orb", "slab", None, None), P("orb", None))
    return jax.shard_map(
        functools.partial(local, n_orb=mesh.shape["orb"], n_slab=mesh.shape["slab"]),
        mesh=mesh, in_specs=placed, out_specs=P("orb", "slab", None, None), check_vma=False
    )
```

time: 151 us -> 103 us (0.68)
  Pallas kernels: 132 us -> 101 us
  blocking collectives: 6.61 us -> 0 us
  other arithmetic: 5.19 us -> 0 us
  local copies, waits for them, and re-layouts: 6.58 us -> 1.89 us
    pallas_call x4 -> x1, Pallas kernels: 132 us -> 101 us  [local(): pl.pallas_call(functools.partial(action_kernel, n_orb, n_slab, half, slot...]
    psum x1 -> x0, blocking collectives: 6.61 us -> none  [local(): both = lax.psum(lanes(jnp.stack([straight, across])) / cell_count, 'slab')]
    slice x4 -> x0, local copies, waits for them, and re-layouts: 2.77 us -> none  [the longest x2 1.75 us: swap(): values[..., grid_len:]]
    reduce_sum x4 -> x0, other arithmetic: 1.72 us -> none  [the longest x1 0.75 us: local(): kept = jnp.sum(both[0][:, :, None, :] * basis[None], axis=1)]
where the time goes in v2:
time: 103 us
  Pallas kernels  101 us (98%)
  local copies, waits for them, and re-layouts  1.89 us (2%)
    pallas_call x1, Pallas kernels, local(): pl.pallas_call(functools.partial(action_kernel, n_orb, n_slab, half, slot...  101 us

profile of v2, /device:TPU:0, one launch (start us, length us, event | category | flops | bytes accessed | tf_op | source)
XLA Modules:
  0.0 103.1 jit_solution(5874965154908909450)
XLA Ops:
  0.0 101.2 %shard_map.46 = f32[1,1024,128]{2,1,0:T(8,128)} custom-call(s32[3,8]{1,0:T(4,128)} %bitcast.5, bf16[1,1024,128]{2,1,0:T(8,128)(2,1)} %bitcast.4, bf16[256,256]{1,0:T(8,128)(2,1)} %constant.5.clone.depth_ref, bf16[64,192]{1,0:T(8,128)(2,1)} %constant.4.clone.turn_ref), custom_call_target="tpu_custom_call" | custom-call | tf_op jit(solution)/shard_map/pallas_call | solution.py:433
  101.2 1.9 %copy.6 = f32[1,16,64,128]{3,2,1,0:T(8,128)} copy(f32[1,16,64,128]{3,2,1,0:T(8,128)} %bitcast.3) | data formatting | bytes 1048576

commit v3 on v2

--- a/solution.py
+++ b/solution.py
@@ -12,6 +12,8 @@
 exchange_fraction = 0.25
 cell_ratio = 8.0
 lines_own = 8
+cube = 16
+batch = 3
 code_peak = 32760.0
 MESH = pl.DeviceIdType.MESH
 VMEM_SPEC = pl.BlockSpec(memory_space=pltpu.VMEM)
@@ -43,16 +45,16 @@
     return both[:, :width] + both[:, width:]
 
 
-def pair_turn(first, second, left_ref):
-    high, low = split(jnp.concatenate([first, second], axis=1))
+def left_turn(fields, left_ref):
+    high, low = split(jnp.concatenate(fields, axis=1))
     return jnp.dot(left_ref[...], jnp.concatenate([high, low, high], axis=0),
                    preferred_element_type=f32)
 
 
 def encode(block):
     peak = jnp.max(jnp.abs(block), axis=0, keepdims=True)
-    inverse = jnp.where(peak > 1e-34, code_peak / jnp.maximum(peak, 1e-34), 0.0)
-    return jnp.round(block * inverse).astype(jnp.int32).astype(jnp.int16), peak * (1.0 / code_peak)
+    unit = (jnp.maximum(peak, 1e-30) * (1.004 / code_peak)).astype(jnp.bfloat16).astype(f32)
+    return jnp.round(block * (1.0 / unit)).astype(jnp.int32).astype(jnp.int16), unit
 
 
 def decode(code, unit):
@@ -64,12 +66,12 @@
                                         device_id=device, device_id_type=MESH)
 
 
-def action_kernel(n_orb, n_slab, half, slots, chunks, grid_len, table_ref, own_ref, depth_ref,
+def action_kernel(n_orb, n_slab, half, quota, chunks, grid_len, table_ref, own_ref, depth_ref,
                   turn_ref, out_ref, *scratch):
     held = scratch[:chunks]
-    (tab_own, tables, tab_s, starts, ids, chosen, gain, kern, fsend, funit, frecv, frunit, work, turned,
-     bsend, bunit, brecv, brunit, terms, parts, rsend, runit, rrecv, rrunit, sums, overlap, overlap_in,
-     coef, ysend,
+    (tab_own, tables, tab_s, starts, ids, chosen, gain, kern, units, fsend, funit, frecv, frunit, frunit_f, work,
+     turned, bsend, bunit, bunit_f, brecv, brunit, terms, parts, rsend, runit, rrecv, rrunit, sums, overlap, packed,
+     packed_in, coef, ysend,
      tab_sem, tab_send, tab_recv, own_sem, g_send, g_recv, stay_sem, f_send, f_recv, keep_sem, b_send,
      b_recv, r_send, r_recv, p_send, p_recv, y_send, y_recv) = scratch[chunks:]
     me, me_slab = lax.axis_index("orb"), lax.axis_index("slab")
@@ -80,10 +82,18 @@
     couples = n_orb * own_couples
     shared = half * own_couples
     capacity = table_ref.shape[1]
-    lines = grid_len // members
+    lines = lines_own
+    bands = grid_len // lines
+    sets = members // bands
+    slots = sets * quota
     planes = grid_len // members // chunks
     rows = planes * grid_len
     tile = planes * lines
+
+    def taker(which, band):
+        return (band // half * sets + which) * half + band % half
+
+    my_band = me_slab // sets * half + part
 
     def line_peer(step):
         return {"orb": lax.rem(me + step, n_orb)}
@@ -153,11 +163,11 @@
         device = {"orb": to * half + part}
         return (remote(rsend.at[chunk, theirs], rrecv.at[chunk, step - 1], r_send.at[0, chunk, step - 1],
                        r_recv.at[0, chunk, step - 1], device),
-                remote(runit.at[chunk, theirs], rrunit.at[chunk, step - 1], r_send.at[1, chunk, step - 1],
+                remote(runit.at[chunk, to], rrunit.at[chunk, step - 1], r_send.at[1, chunk, step - 1],
                        r_recv.at[1, chunk, step - 1], device))
 
     def overlap_copy(step):
-        return remote(overlap, overlap_in.at[step - 1], p_send.at[step - 1], p_recv.at[step - 1],
+        return remote(packed, packed_in.at[step - 1], p_send.at[step - 1], p_recv.at[step - 1],
                       member(step)[1])
 
     def result_copy(chunk, hop):
@@ -186,18 +196,17 @@
     fx = cell_ratio * fy
     scale_k = (2.0 * math.pi / grid_len) * (2.0 * math.pi / grid_len)
     for line in range(lines):
-        at = place * lines + line
+        at = my_band * lines + line
         fl = jnp.minimum(at, grid_len - at).astype(f32)
         plane = fl * fl + fz * fz
         whole = fx * fx + plane
         level = jnp.where(plane > 0, plane, deep)
-        kern[line * grid_len:(line + 1) * grid_len] = jnp.where(
+        kern[:, line * width:(line + 1) * width] = jnp.where(
             whole > 0, (-exchange_fraction / scale_k) * level / jnp.where(whole > 0, whole, 1.0), 0.0)
     terms[2 * slots] = jnp.zeros(terms.shape[1:], f32)
     overlap[...] = jnp.zeros(overlap.shape, f32)
-    for chunk in range(chunks):
-        for ref in (funit, bunit):
-            ref[chunk] = jnp.zeros(ref.shape[1:], f32)
+    units[...] = jnp.zeros(units.shape, f32)
+    runit[...] = jnp.zeros(runit.shape, f32)
 
     for step in range(1, n_orb):
         tab_copy(step).wait_recv()
@@ -240,18 +249,24 @@
         for step in range(1, n_orb):
             gather_copy(chunk, step).wait_recv()
 
-        @pl.loop(0, slots)
-        def _(slot):
-            left, partner, _ = pair_of(chunk, slot)
-            flat = depth_turn(left * partner, depth_ref)
-            done = pair_turn(flat[:grid_len], flat[grid_len:], turn_ref)
-            one, two = done[:, :width] * gain[...], done[:, width:] * gain[...]
-            for to in range(members):
-                span = slice(to * lines, (to + 1) * lines)
-                code, unit = encode(jnp.concatenate([one[span], two[span]], axis=0))
-                fsend[chunk, to, slot] = code
-                funit[chunk, to, pl.ds(slot, 1)] = unit
-
+        for which in range(sets):
+            @pl.loop(0, quota, step=batch)
+            def _(base):
+                pairs = [pair_of(chunk, which * quota + base + k) for k in range(batch)]
+                flat = depth_turn(jnp.concatenate([left * partner for left, partner, _ in pairs], axis=0),
+                                  depth_ref)
+                done = left_turn([flat[k * grid_len:(k + 1) * grid_len] for k in range(2 * batch)], turn_ref)
+                for k in range(batch):
+                    one = done[:, 2 * k * width:(2 * k + 1) * width] * gain[...]
+                    two = done[:, (2 * k + 1) * width:(2 * k + 2) * width] * gain[...]
+                    for band in range(bands):
+                        to = taker(which, band)
+                        span = slice(band * lines, (band + 1) * lines)
+                        code, unit = encode(jnp.concatenate([one[span], two[span]], axis=0))
+                        fsend[chunk, to, base + k] = code
+                        units[to, pl.ds(base + k, 1)] = unit
+
+        funit[chunk] = units[...].astype(funit.dtype)
         for step in range(1, members):
             for copy in fwd_copies(chunk, step):
                 copy.start()
@@ -268,26 +283,31 @@
             for copy in fwd_copies(chunk, step):
                 copy.wait_recv()
 
-    @pl.loop(0, slots)
-    def _(slot):
-        for src in range(members):
-            for chunk in range(chunks):
-                at = (src * chunks + chunk) * tile
-                work[at:at + tile] = decode(frecv[slot, src, chunk], frunit[src, chunk, pl.ds(slot, 1)])
-        for line in range(0, lines, 2):
-            one, two = pl.ds(line, grid_len, stride=lines), pl.ds(line + 1, grid_len, stride=lines)
-            low, mid, high = line * grid_len, (line + 1) * grid_len, (line + 2) * grid_len
-            done = pair_turn(work[one, :], work[two, :], turn_ref)
-            back = pair_turn(done[:, :width] * kern[low:mid], done[:, width:] * kern[mid:high], turn_ref)
-            turned[one, :] = back[:, :width]
-            turned[two, :] = back[:, width:]
-        for to in range(members):
-            for chunk in range(chunks):
-                at = (to * chunks + chunk) * tile
-                code, unit = encode(turned[at:at + tile])
-                bsend[chunk, to, slot] = code
-                bunit[chunk, to, pl.ds(slot, 1)] = unit
-
+    for chunk in range(chunks):
+        frunit_f[:, chunk] = frunit[:, chunk].astype(f32)
+
+    @pl.loop(0, quota, step=batch)
+    def _(base):
+        for k in range(batch):
+            for src in range(members):
+                for chunk in range(chunks):
+                    at = (src * chunks + chunk) * tile
+                    work[k, at:at + tile] = decode(frecv[base + k, src, chunk],
+                                                   frunit_f[src, chunk, pl.ds(base + k, 1)])
+            done = left_turn([work[k, pl.ds(line, grid_len, stride=lines), :] for line in range(lines)],
+                             turn_ref)
+            done = done * kern[...]
+            back = left_turn([done[:, line * width:(line + 1) * width] for line in range(lines)], turn_ref)
+            for line in range(lines):
+                turned[k, pl.ds(line, grid_len, stride=lines), :] = back[:, line * width:(line + 1) * width]
+            for to in range(members):
+                for chunk in range(chunks):
+                    at = (to * chunks + chunk) * tile
+                    code, unit = encode(turned[k, at:at + tile])
+                    bsend[chunk, to, base + k] = code
+                    bunit_f[chunk, to, pl.ds(base + k, 1)] = unit
+
+    bunit[...] = bunit_f[...].astype(bunit.dtype)
     for chunk in range(chunks):
         for step in range(1, members):
             for copy in back_copies(chunk, step):
@@ -302,17 +322,28 @@
             for copy in back_copies(chunk, step):
                 copy.wait_recv()
 
-        @pl.loop(0, slots)
-        def _(slot):
-            blocks = [decode(brecv[chunk, src, slot], brunit[chunk, src, pl.ds(slot, 1)])
-                      for src in range(members)]
-            done = pair_turn(jnp.concatenate([block[:lines] for block in blocks], axis=0),
-                             jnp.concatenate([block[lines:] for block in blocks], axis=0), turn_ref)
-            potential = depth_turn(jnp.concatenate([done[:, :width], done[:, width:]], axis=0), depth_ref)
-            left, partner, flipped = pair_of(chunk, slot)
-            terms[2 * slot] = potential * partner
-            second = potential * left
-            terms[2 * slot + 1] = jnp.where(flipped, pltpu.roll(second, grid_len, 1), second)
+        units[...] = brunit[chunk].astype(f32)
+
+        for which in range(sets):
+            @pl.loop(0, quota, step=batch)
+            def _(base):
+                fields = []
+                for k in range(batch):
+                    blocks = [decode(brecv[chunk, taker(which, band), base + k],
+                                     units[taker(which, band), pl.ds(base + k, 1)])
+                              for band in range(bands)]
+                    fields.append(jnp.concatenate([block[:lines] for block in blocks], axis=0))
+                    fields.append(jnp.concatenate([block[lines:] for block in blocks], axis=0))
+                done = left_turn(fields, turn_ref)
+                potentials = depth_turn(jnp.concatenate(
+                    [done[:, k * width:(k + 1) * width] for k in range(2 * batch)], axis=0), depth_ref)
+                for k in range(batch):
+                    slot = which * quota + base + k
+                    potential = potentials[k * rows:(k + 1) * rows]
+                    left, partner, flipped = pair_of(chunk, slot)
+                    terms[2 * slot] = potential * partner
+                    second = potential * left
+                    terms[2 * slot + 1] = jnp.where(flipped, pltpu.roll(second, grid_len, 1), second)
 
         @pl.loop(0, couples)
         def _(couple):
@@ -322,7 +353,7 @@
             parts[chunk, couple] = total
             code, unit = encode(total)
             rsend[chunk, couple] = code
-            runit[chunk, couple] = jnp.broadcast_to(unit, runit.shape[2:])
+            runit[chunk, couple // shared, pl.ds(couple % shared, 1)] = unit
 
         for step in range(1, groups):
             for copy in sum_copies(chunk, step):
@@ -335,7 +366,7 @@
         for k in range(shared):
             total = parts[chunk, group * shared + k]
             for step in range(1, groups):
-                total = total + decode(rrecv[chunk, step - 1, k], rrunit[chunk, step - 1, k, 0:1])
+                total = total + decode(rrecv[chunk, step - 1, k], rrunit[chunk, step - 1, k:k + 1])
             sums[chunk, k] = total
             across = pltpu.roll(total, grid_len, 1)
 
@@ -352,17 +383,26 @@
             collect(chunk - 1)
     collect(chunks - 1)
 
+    lane = lax.broadcasted_iota(jnp.int32, (8, width), 1)
+    halves = ((lane // grid_len) == lax.broadcasted_iota(jnp.int32, (8, width), 0)).astype(jnp.bfloat16)
+
+    def thirds(values):
+        high = values.astype(jnp.bfloat16)
+        rest = values - high.astype(f32)
+        mid = rest.astype(jnp.bfloat16)
+        return high, mid, (rest - mid.astype(f32)).astype(jnp.bfloat16)
+
+    packed[...] = sum(lax.dot_general(halves, third, (((1,), (1,)), ((), ())), preferred_element_type=f32)
+                      for third in thirds(overlap[...]))
     for step in range(1, members):
         overlap_copy(step).start()
-    total = overlap[...]
+    total = packed[...]
     for step in range(1, members):
         overlap_copy(step).wait_recv()
-        total = total + overlap_in[step - 1]
+        total = total + packed_in[step - 1]
     total = total * (1.0 / (grid_len * grid_len * grid_len))
-    lane = lax.broadcasted_iota(jnp.int32, total.shape, 1)
-    lower = jnp.sum(jnp.where(lane < grid_len, total, 0.0), axis=1, keepdims=True)
-    upper = jnp.sum(jnp.where(lane < grid_len, 0.0, total), axis=1, keepdims=True)
-    coef[...] = jnp.where(lane < grid_len, lower, upper)
+    coef[...] = sum(lax.dot_general(third, halves, (((0,), (0,)), ((), ())), preferred_element_type=f32)
+                    for third in thirds(total))
 
     strip = rows // 4
     for chunk in range(chunks):
@@ -403,16 +443,21 @@
 def local(orbitals, pair_table, n_orb, n_slab):
     own_couples, slab_len, grid_len, width = orbitals.shape
     capacity = pair_table.shape[0]
-    half = max(1, grid_len // (lines_own * n_slab))
+    half = max(1, cube // n_slab)
     members = n_slab * half
     groups = n_orb // half
+    bands = grid_len // lines_own
+    sets = members // bands
     live_total = sum(capacity * (k + 1) // n_orb for k in range(n_orb))
-    slots = -(-live_total // groups)
+    quota = -(-live_total // (groups * sets * batch)) * batch
+    slots = sets * quota
     couples, shared = n_orb * own_couples, half * own_couples
-    lines = grid_len // members
-    chunks = lines // 2
-    rows, tile = 2 * grid_len, 2 * lines
-    slots_pad = -(-slots // 8) * 8
+    planes = grid_len // members
+    chunks = planes // 2
+    rows, tile = 2 * grid_len, 2 * lines_own
+    quota_pad = -(-quota // 16) * 16
+    shared_pad = -(-shared // 8) * 8
+    overlap_rows = -(-2 * shared * couples // 128) * 128
     tab_lanes = -(-capacity // 128) * 128
 
     mat = hartley(grid_len)
@@ -423,34 +468,35 @@
 
     dma, vmem, smem = pltpu.SemaphoreType.DMA, pltpu.VMEM, pltpu.SMEM
     i32, i16 = jnp.int32, jnp.int16
-    coded = vmem((chunks, members, slots, tile, width), i16)
-    units = vmem((chunks, members, slots_pad, width), f32)
+    bf16 = orbitals.dtype
+    coded = vmem((chunks, members, quota, tile, width), i16)
+    sent_units = vmem((chunks, members, quota_pad, width), bf16)
     lines_sem = dma((chunks, n_orb - 1))
     cross_sem = dma((2, chunks, members - 1))
     steps = max(groups - 1, 1)
     sum_sem = dma((2, chunks, steps))
     hops = max(half - 1, 1)
     out = pl.pallas_call(
-        functools.partial(action_kernel, n_orb, n_slab, half, slots, chunks, grid_len),
+        functools.partial(action_kernel, n_orb, n_slab, half, quota, chunks, grid_len),
         out_shape=jax.ShapeDtypeStruct((own_couples, slab_len * grid_len, width), f32),
         in_specs=[VMEM_SPEC] * 4,
         out_specs=VMEM_SPEC,
         scratch_shapes=[vmem((couples, rows, width), orbitals.dtype)] * chunks + [
             vmem((8, tab_lanes), i32), vmem((n_orb, 8, tab_lanes), i32), smem((n_orb, 8, tab_lanes), i32),
             smem((n_orb,), i32), smem((slots, 3), i32), smem((couples, slots), i32),
-            vmem((grid_len, width), f32), vmem((lines * grid_len, width), f32),
-            coded, units,
-            vmem((slots, members, chunks, tile, width), i16), vmem((members, chunks, slots_pad, width), f32),
-            vmem((lines * grid_len, width), f32), vmem((lines * grid_len, width), f32),
-            coded, units, coded, units,
+            vmem((grid_len, width), f32), vmem((grid_len, lines_own * width), f32),
+            vmem((members, quota_pad, width), f32), coded, sent_units,
+            vmem((quota, members, chunks, tile, width), i16), vmem((members, chunks, quota_pad, width), bf16),
+            vmem((members, chunks, quota_pad, width), f32),
+            vmem((batch, lines_own * grid_len, width), f32), vmem((batch, lines_own * grid_len, width), f32),
+            coded, sent_units, vmem((chunks, members, quota_pad, width), f32), coded, sent_units,
             vmem((2 * slots + 1, rows, width), f32),
             vmem((chunks, couples, rows, width), f32),
-            vmem((chunks, couples, rows, width), i16), vmem((chunks, couples, 8, width), f32),
-            vmem((chunks, steps, shared, rows, width), i16), vmem((chunks, steps, shared, 8, width), f32),
+            vmem((chunks, couples, rows, width), i16), vmem((chunks, groups, shared_pad, width), f32),
+            vmem((chunks, steps, shared, rows, width), i16), vmem((chunks, steps, shared_pad, width), f32),
             vmem((chunks, shared, rows, width), f32),
-            vmem((2 * shared * couples, width), f32),
-            vmem((members - 1, 2 * shared * couples, width), f32),
-            vmem((2 * shared * couples, width), f32),
+            vmem((overlap_rows, width), f32), vmem((8, overlap_rows), f32),
+            vmem((members - 1, 8, overlap_rows), f32), vmem((overlap_rows, width), f32),
             vmem((chunks, shared, rows, width), f32),
             dma, dma((n_orb - 1,)), dma((n_orb - 1,)), dma((chunks,)), lines_sem, lines_sem,
             dma((2, chunks)), cross_sem, cross_sem, dma((2, chunks)), cross_sem, cross_sem,

time: 103 us -> 84.8 us (0.82)
  Pallas kernels: 101 us -> 82.7 us
    pallas_call x1, Pallas kernels: 101 us -> 82.7 us  [local(): pl.pallas_call(functools.partial(action_kernel, n_orb, n_slab, half, quot...]
where the time goes in v3:
time: 84.8 us; the launch traced here: 84.6 us
  Pallas kernels  82.7 us (98%)
  local copies, waits for them, and re-layouts  1.89 us (2%)
    pallas_call x1, Pallas kernels, local(): pl.pallas_call(functools.partial(action_kernel, n_orb, n_slab, half, quot...  82.7 us
    unnamed x1, local copies, waits for them, and re-layouts  1.89 us

profile of v3, /device:TPU:0, one launch (start us, length us, event | category | flops | bytes accessed | tf_op | source)
XLA Modules:
  0.0 84.6 jit_solution(11102989745331503400)
XLA Ops:
  0.0 82.7 %shard_map.46 = f32[1,1024,128]{2,1,0:T(8,128)} custom-call(s32[3,8]{1,0:T(4,128)} %bitcast.5, bf16[1,1024,128]{2,1,0:T(8,128)(2,1)} %bitcast.4, bf16[256,256]{1,0:T(8,128)(2,1)} %constant.5.clone.depth_ref, bf16[64,192]{1,0:T(8,128)(2,1)} %constant.4.clone.turn_ref), custom_call_target="tpu_custom_call" | custom-call | tf_op jit(solution)/shard_map/pallas_call | solution.py:479
  82.7 1.9 %copy.6 = f32[1,16,64,128]{3,2,1,0:T(8,128)} copy(f32[1,16,64,128]{3,2,1,0:T(8,128)} %bitcast.3) | data formatting | bytes 1048576

commit v4 on v3

--- a/solution.py
+++ b/solution.py
@@ -67,13 +67,13 @@
 
 
 def action_kernel(n_orb, n_slab, half, quota, chunks, grid_len, table_ref, own_ref, depth_ref,
-                  turn_ref, out_ref, *scratch):
+                  turn_ref, out_ref, unit_ref, *scratch):
     held = scratch[:chunks]
     (tab_own, tables, tab_s, starts, ids, chosen, gain, kern, units, fsend, funit, frecv, frunit, frunit_f, work,
-     turned, bsend, bunit, bunit_f, brecv, brunit, terms, parts, rsend, runit, rrecv, rrunit, sums, overlap, packed,
-     packed_in, coef, ysend,
+     turned, bsend, bunit, bunit_f, brecv, brunit, terms, parts, rsend, runit, rrecv, rrunit, overlap, packed,
+     packed_in, merged, merged_in, coef, result, ysend, yunit,
      tab_sem, tab_send, tab_recv, own_sem, g_send, g_recv, stay_sem, f_send, f_recv, keep_sem, b_send,
-     b_recv, r_send, r_recv, p_send, p_recv, y_send, y_recv) = scratch[chunks:]
+     b_recv, r_send, r_recv, o_send, o_recv, p_send, p_recv, y_send, y_recv) = scratch[chunks:]
     me, me_slab = lax.axis_index("orb"), lax.axis_index("slab")
     group, part = me // half, me % half
     groups, members = n_orb // half, n_slab * half
@@ -86,6 +86,7 @@
     bands = grid_len // lines
     sets = members // bands
     slots = sets * quota
+    runs = quota // batch
     planes = grid_len // members // chunks
     rows = planes * grid_len
     tile = planes * lines
@@ -111,7 +112,6 @@
                 barrier, inc=1, device_id={"orb": group * half + other,
                                            "slab": lax.rem(me_slab + slab_step, n_slab)},
                 device_id_type=MESH)
-    pl.semaphore_wait(barrier, n_orb - 1 + (n_slab - 1) * half)
 
     def plane_rows(which, chunk):
         return pl.ds(pl.multiple_of((which * chunks + chunk) * rows, rows), rows)
@@ -131,12 +131,15 @@
                                      held[chunk].at[pl.ds(me * own_couples, own_couples)],
                                      own_sem.at[chunk])
 
-    def fwd_copies(chunk, step):
+    def fwd_copy(chunk, step):
         to, device = member(step)
-        return (remote(fsend.at[chunk, to], frecv.at[:, place, chunk], f_send.at[0, chunk, step - 1],
-                       f_recv.at[0, chunk, step - 1], device),
-                remote(funit.at[chunk, to], frunit.at[place, chunk], f_send.at[1, chunk, step - 1],
-                       f_recv.at[1, chunk, step - 1], device))
+        return remote(fsend.at[chunk, to], frecv.at[:, place, chunk], f_send.at[0, chunk, step - 1],
+                      f_recv.at[0, chunk, step - 1], device)
+
+    def fwd_unit(chunk, step):
+        to, device = member(step)
+        return remote(funit.at[chunk, to], frunit.at[place, chunk], f_send.at[1, chunk, step - 1],
+                      f_recv.at[1, chunk, step - 1], device)
 
     def fwd_stay(chunk):
         return (pltpu.make_async_copy(fsend.at[chunk, place], frecv.at[:, place, chunk],
@@ -144,12 +147,16 @@
                 pltpu.make_async_copy(funit.at[chunk, place], frunit.at[place, chunk],
                                       stay_sem.at[1, chunk]))
 
-    def back_copies(chunk, step):
+    def back_copy(chunk, step, run):
         to, device = member(step)
-        return (remote(bsend.at[chunk, to], brecv.at[chunk, place], b_send.at[0, chunk, step - 1],
-                       b_recv.at[0, chunk, step - 1], device),
-                remote(bunit.at[chunk, to], brunit.at[chunk, place], b_send.at[1, chunk, step - 1],
-                       b_recv.at[1, chunk, step - 1], device))
+        some = pl.ds(run * batch, batch)
+        return remote(bsend.at[chunk, to, some], brecv.at[chunk, place, some],
+                      b_send.at[run, chunk, step - 1], b_recv.at[run, chunk, step - 1], device)
+
+    def back_unit(chunk, step):
+        to, device = member(step)
+        return remote(bunit.at[chunk, to], brunit.at[chunk, place], b_send.at[runs, chunk, step - 1],
+                      b_recv.at[runs, chunk, step - 1], device)
 
     def back_stay(chunk):
         return (pltpu.make_async_copy(bsend.at[chunk, place], brecv.at[chunk, place],
@@ -167,25 +174,24 @@
                        r_recv.at[1, chunk, step - 1], device))
 
     def overlap_copy(step):
-        return remote(packed, packed_in.at[step - 1], p_send.at[step - 1], p_recv.at[step - 1],
+        to = lax.rem(group + step, groups)
+        return remote(packed.at[to], packed_in.at[step - 1], o_send.at[step - 1], o_recv.at[step - 1],
+                      {"orb": to * half + part})
+
+    def merged_copy(step):
+        return remote(merged, merged_in.at[step - 1], p_send.at[step - 1], p_recv.at[step - 1],
                       member(step)[1])
 
-    def result_copy(chunk, hop):
+    def result_copies(chunk, hop):
         to = lax.rem(part + hop, half)
-        return remote(ysend.at[chunk, pl.ds(to * own_couples, own_couples)],
-                      out_ref.at[:, plane_rows(part, chunk)], y_send.at[chunk, hop - 1],
-                      y_recv.at[chunk, hop - 1], {"orb": group * half + to})
+        theirs, device = pl.ds(to * own_couples, own_couples), {"orb": group * half + to}
+        return (remote(ysend.at[chunk, theirs], out_ref.at[:, plane_rows(part, chunk)],
+                       y_send.at[0, chunk, hop - 1], y_recv.at[0, chunk, hop - 1], device),
+                remote(yunit.at[chunk, theirs], unit_ref.at[:, part * chunks + chunk],
+                       y_send.at[1, chunk, hop - 1], y_recv.at[1, chunk, hop - 1], device))
 
     tab_own[...] = jnp.full(tab_own.shape, -1, jnp.int32)
     tab_own[0:3, 0:capacity] = table_ref[...]
-    for step in range(1, n_orb):
-        tab_copy(step).start()
-    for chunk in range(chunks):
-        for step in range(1, n_orb):
-            gather_copy(chunk, step).start()
-        own_copy(chunk).start()
-    tables[me] = tab_own[...]
-
     kz = lax.broadcasted_iota(jnp.int32, (grid_len, width), 1) % grid_len
     fz = jnp.minimum(kz, grid_len - kz).astype(f32)
     ky = lax.broadcasted_iota(jnp.int32, (grid_len, width), 0)
@@ -208,6 +214,15 @@
     units[...] = jnp.zeros(units.shape, f32)
     runit[...] = jnp.zeros(runit.shape, f32)
 
+    pl.semaphore_wait(barrier, n_orb - 1 + (n_slab - 1) * half)
+    for step in range(1, n_orb):
+        tab_copy(step).start()
+    for chunk in range(chunks):
+        for step in range(1, n_orb):
+            gather_copy(chunk, step).start()
+        own_copy(chunk).start()
+    tables[me] = tab_own[...]
+
     for step in range(1, n_orb):
         tab_copy(step).wait_recv()
     to_scalars = pltpu.make_async_copy(tables, tab_s, tab_sem)
@@ -266,10 +281,16 @@
                         fsend[chunk, to, base + k] = code
                         units[to, pl.ds(base + k, 1)] = unit
 
+            for step in range(1, members):
+                to = member(step)[0]
+
+                @pl.when(to // half % sets == which)
+                def _():
+                    fwd_copy(chunk, step).start()
+
         funit[chunk] = units[...].astype(funit.dtype)
         for step in range(1, members):
-            for copy in fwd_copies(chunk, step):
-                copy.start()
+            fwd_unit(chunk, step).start()
         for copy in fwd_stay(chunk):
             copy.start()
 
@@ -280,8 +301,8 @@
         for copy in fwd_stay(chunk):
             copy.wait()
         for step in range(1, members):
-            for copy in fwd_copies(chunk, step):
-                copy.wait_recv()
+            fwd_copy(chunk, step).wait_recv()
+            fwd_unit(chunk, step).wait_recv()
 
     for chunk in range(chunks):
         frunit_f[:, chunk] = frunit[:, chunk].astype(f32)
@@ -306,12 +327,17 @@
                     code, unit = encode(turned[k, at:at + tile])
                     bsend[chunk, to, base + k] = code
                     bunit_f[chunk, to, pl.ds(base + k, 1)] = unit
+        for step in range(1, members):
+            back_copy(0, step, base // batch).start()
 
     bunit[...] = bunit_f[...].astype(bunit.dtype)
     for chunk in range(chunks):
         for step in range(1, members):
-            for copy in back_copies(chunk, step):
-                copy.start()
+            back_unit(chunk, step).start()
+        if chunk:
+            for run in range(runs):
+                for step in range(1, members):
+                    back_copy(chunk, step, run).start()
         for copy in back_stay(chunk):
             copy.start()
 
@@ -319,8 +345,9 @@
         for copy in back_stay(chunk):
             copy.wait()
         for step in range(1, members):
-            for copy in back_copies(chunk, step):
-                copy.wait_recv()
+            for run in range(runs):
+                back_copy(chunk, step, run).wait_recv()
+            back_unit(chunk, step).wait_recv()
 
         units[...] = brunit[chunk].astype(f32)
 
@@ -354,34 +381,21 @@
             code, unit = encode(total)
             rsend[chunk, couple] = code
             runit[chunk, couple // shared, pl.ds(couple % shared, 1)] = unit
-
+            across = pltpu.roll(total, grid_len, 1)
+            at = couple % shared * couples
+            for other in range(couples):
+                basis = held[chunk][other].astype(f32)
+                for kind, field in enumerate((total, across)):
+                    row = pl.ds(at + kind * shared * couples + other, 1)
+                    overlap[couple // shared, row] += jnp.sum(basis * field, axis=0, keepdims=True)
+
+
+    for chunk in range(chunks - 1):
+        retreat(chunk)
         for step in range(1, groups):
             for copy in sum_copies(chunk, step):
                 copy.start()
-
-    def collect(chunk):
-        for step in range(1, groups):
-            for copy in sum_copies(chunk, step):
-                copy.wait_recv()
-        for k in range(shared):
-            total = parts[chunk, group * shared + k]
-            for step in range(1, groups):
-                total = total + decode(rrecv[chunk, step - 1, k], rrunit[chunk, step - 1, k:k + 1])
-            sums[chunk, k] = total
-            across = pltpu.roll(total, grid_len, 1)
-
-            @pl.loop(0, couples)
-            def _(couple):
-                basis = held[chunk][couple].astype(f32)
-                for kind, field in enumerate((total, across)):
-                    at = pl.ds((kind * shared + k) * couples + couple, 1)
-                    overlap[at] += jnp.sum(basis * field, axis=0, keepdims=True)
-
-    for chunk in range(chunks):
-        retreat(chunk)
-        if chunk:
-            collect(chunk - 1)
-    collect(chunks - 1)
+    retreat(chunks - 1)
 
     lane = lax.broadcasted_iota(jnp.int32, (8, width), 1)
     halves = ((lane // grid_len) == lax.broadcasted_iota(jnp.int32, (8, width), 0)).astype(jnp.bfloat16)
@@ -392,20 +406,35 @@
         mid = rest.astype(jnp.bfloat16)
         return high, mid, (rest - mid.astype(f32)).astype(jnp.bfloat16)
 
-    packed[...] = sum(lax.dot_general(halves, third, (((1,), (1,)), ((), ())), preferred_element_type=f32)
-                      for third in thirds(overlap[...]))
-    for step in range(1, members):
+    for which in range(groups):
+        packed[which] = sum(lax.dot_general(halves, third, (((1,), (1,)), ((), ())),
+                                            preferred_element_type=f32)
+                            for third in thirds(overlap[which]))
+    for step in range(1, groups):
         overlap_copy(step).start()
-    total = packed[...]
-    for step in range(1, members):
+    for step in range(1, groups):
+        for copy in sum_copies(chunks - 1, step):
+            copy.start()
+    total = packed[group]
+    for step in range(1, groups):
         overlap_copy(step).wait_recv()
         total = total + packed_in[step - 1]
+    merged[...] = total
+    for step in range(1, members):
+        merged_copy(step).start()
+    for step in range(1, members):
+        merged_copy(step).wait_recv()
+        total = total + merged_in[step - 1]
     total = total * (1.0 / (grid_len * grid_len * grid_len))
     coef[...] = sum(lax.dot_general(third, halves, (((0,), (0,)), ((), ())), preferred_element_type=f32)
                     for third in thirds(total))
 
     strip = rows // 4
     for chunk in range(chunks):
+        for step in range(1, groups):
+            for copy in sum_copies(chunk, step):
+                copy.wait_recv()
+
         @pl.loop(0, rows // strip)
         def _(at):
             here = pl.ds(pl.multiple_of(at * strip, strip), strip)
@@ -416,26 +445,42 @@
                     row = k * couples + couple
                     kept[k] = kept[k] + coef[row:row + 1] * basis
             for k in range(shared):
-                ysend[chunk, k, here] = (sums[chunk, k, here] - kept[k]
-                                         - pltpu.roll(kept[shared + k], grid_len, 1))
-
+                total = parts[chunk, group * shared + k, here]
+                for step in range(1, groups):
+                    total = total + decode(rrecv[chunk, step - 1, k, here],
+                                           rrunit[chunk, step - 1, k:k + 1])
+                result[k, here] = total - kept[k] - pltpu.roll(kept[shared + k], grid_len, 1)
+
+        for k in range(shared):
+            code, unit = encode(result[k])
+            ysend[chunk, k] = code
+            yunit[chunk, k] = jnp.broadcast_to(unit, yunit.shape[2:])
         for hop in range(1, half):
-            result_copy(chunk, hop).start()
-        out_ref[:, plane_rows(part, chunk)] = ysend[chunk, pl.ds(part * own_couples, own_couples)]
+            for copy in result_copies(chunk, hop):
+                copy.start()
+        mine = pl.ds(part * own_couples, own_couples)
+        out_ref[:, plane_rows(part, chunk)] = ysend[chunk, mine]
+        unit_ref[:, part * chunks + chunk] = yunit[chunk, mine]
 
     for chunk in range(chunks):
         for hop in range(1, half):
-            result_copy(chunk, hop).wait()
+            for copy in result_copies(chunk, hop):
+                copy.wait()
         for step in range(1, members):
-            for copy in fwd_copies(chunk, step) + back_copies(chunk, step):
-                copy.wait_send()
+            fwd_copy(chunk, step).wait_send()
+            fwd_unit(chunk, step).wait_send()
+            for run in range(runs):
+                back_copy(chunk, step, run).wait_send()
+            back_unit(chunk, step).wait_send()
         for step in range(1, groups):
             for copy in sum_copies(chunk, step):
                 copy.wait_send()
         for step in range(1, n_orb):
             gather_copy(chunk, step).wait_send()
+    for step in range(1, groups):
+        overlap_copy(step).wait_send()
     for step in range(1, members):
-        overlap_copy(step).wait_send()
+        merged_copy(step).wait_send()
     for step in range(1, n_orb):
         tab_copy(step).wait_send()
 
@@ -473,14 +518,17 @@
     sent_units = vmem((chunks, members, quota_pad, width), bf16)
     lines_sem = dma((chunks, n_orb - 1))
     cross_sem = dma((2, chunks, members - 1))
+    back_sem = dma((quota // batch + 1, chunks, members - 1))
     steps = max(groups - 1, 1)
     sum_sem = dma((2, chunks, steps))
     hops = max(half - 1, 1)
-    out = pl.pallas_call(
+    blocks = slab_len * grid_len // rows
+    code, unit = pl.pallas_call(
         functools.partial(action_kernel, n_orb, n_slab, half, quota, chunks, grid_len),
-        out_shape=jax.ShapeDtypeStruct((own_couples, slab_len * grid_len, width), f32),
+        out_shape=(jax.ShapeDtypeStruct((own_couples, slab_len * grid_len, width), i16),
+                   jax.ShapeDtypeStruct((own_couples, blocks, 8, width), f32)),
         in_specs=[VMEM_SPEC] * 4,
-        out_specs=VMEM_SPEC,
+        out_specs=(VMEM_SPEC, VMEM_SPEC),
         scratch_shapes=[vmem((couples, rows, width), orbitals.dtype)] * chunks + [
             vmem((8, tab_lanes), i32), vmem((n_orb, 8, tab_lanes), i32), smem((n_orb, 8, tab_lanes), i32),
             smem((n_orb,), i32), smem((slots, 3), i32), smem((couples, slots), i32),
@@ -494,19 +542,21 @@
             vmem((chunks, couples, rows, width), f32),
             vmem((chunks, couples, rows, width), i16), vmem((chunks, groups, shared_pad, width), f32),
             vmem((chunks, steps, shared, rows, width), i16), vmem((chunks, steps, shared_pad, width), f32),
-            vmem((chunks, shared, rows, width), f32),
-            vmem((overlap_rows, width), f32), vmem((8, overlap_rows), f32),
+            vmem((groups, overlap_rows, width), f32), vmem((groups, 8, overlap_rows), f32),
+            vmem((steps, 8, overlap_rows), f32), vmem((8, overlap_rows), f32),
             vmem((members - 1, 8, overlap_rows), f32), vmem((overlap_rows, width), f32),
-            vmem((chunks, shared, rows, width), f32),
+            vmem((shared, rows, width), f32),
+            vmem((chunks, shared, rows, width), i16), vmem((chunks, shared, 8, width), f32),
             dma, dma((n_orb - 1,)), dma((n_orb - 1,)), dma((chunks,)), lines_sem, lines_sem,
-            dma((2, chunks)), cross_sem, cross_sem, dma((2, chunks)), cross_sem, cross_sem,
-            sum_sem, sum_sem, dma((members - 1,)), dma((members - 1,)),
-            dma((chunks, hops)), dma((chunks, hops)),
+            dma((2, chunks)), cross_sem, cross_sem, dma((2, chunks)), back_sem, back_sem,
+            sum_sem, sum_sem, dma((steps,)), dma((steps,)), dma((members - 1,)), dma((members - 1,)),
+            dma((2, chunks, hops)), dma((2, chunks, hops)),
         ],
         compiler_params=pltpu.CompilerParams(collective_id=0, has_side_effects=True,
                                              vmem_limit_bytes=56 << 20),
     )(pair_table.T, orbitals.reshape(own_couples, slab_len * grid_len, width), depth_mat, turn_mat)
-    return out.reshape(orbitals.shape)
+    pieces = code.reshape(own_couples, blocks, rows, width).astype(f32)
+    return (pieces * unit[:, :, :1]).reshape(orbitals.shape)
 
 
 def solution(mesh):

time: 84.8 us -> 79.1 us (0.933)
  Pallas kernels: 82.7 us -> 76.2 us
  other arithmetic: 0 us -> 1.83 us
  local copies, waits for them, and re-layouts: 1.89 us -> 0.77 us
    pallas_call x1, Pallas kernels: 82.7 us -> 76.2 us  [local(): pl.pallas_call(functools.partial(action_kernel, n_orb, n_slab, half, quot...]
    unnamed x1 -> x0, local copies, waits for them, and re-layouts: 1.89 us -> none
    mul x0 -> x1, other arithmetic: none -> 1.83 us  [local(): return (pieces * unit[:, :, :1]).reshape(orbitals.shape)]
where the time goes in v4:
time: 79.1 us; the launch traced here: 78.9 us
  Pallas kernels  76.2 us (96%)
  other arithmetic  1.83 us (2%)
    pallas_call x1, Pallas kernels, local(): pl.pallas_call(functools.partial(action_kernel, n_orb, n_slab, half, quot...  76.2 us
    mul x1, other arithmetic, local(): return (pieces * unit[:, :, :1]).reshape(orbitals.shape)  1.83 us

profile of v4, /device:TPU:0, one launch (start us, length us, event | category | flops | bytes accessed | tf_op | source)
XLA Modules:
  0.0 78.9 jit_solution(535623590186193687)
XLA Ops:
  0.0 76.2 %shard_map.46 = (s16[1,1024,128]{2,1,0:T(8,128)(2,1)}, f32[1,8,8,128]{3,2,1,0:T(8,128)}) custom-call(s32[3,8]{1,0:T(4,128)} %bitcast.10, bf16[1,1024,128]{2,1,0:T(8,128)(2,1)} %bitcast.7, bf16[256,256]{1,0:T(8,128)(2,1)} %constant.5.clone.depth_ref, bf16[64,192]{1,0:T(8,128)(2,1)} %constant.4.clone.turn_ref), custom_call_target="tpu_custom_call" | custom-call | tf_op jit(solution)/shard_map/pallas_call | solution.py:526
  76.3 0.8 slice.3
  77.0 1.8 %convert_multiply_fusion = f32[1,16,64,128]{3,2,1,0:T(8,128)} fusion(s16[1,16,64,128]{3,2,1,0:T(8,128)(2,1)} %bitcast.6, f32[16,128]{1,0:T(8,128)S(1)} %bitcast.8), kind=kLoop, calls=%fused_computation | loop fusion | flops 262144 | bytes 794624 | tf_op jit(solution)/shard_map/mul | solution.py:559
  (1 shorter events, 0.0 us)

commit v5 on v4

v5 whole, which is shorter than its diff:
```python
import functools
import math

import jax
import jax.numpy as jnp
import numpy as np
from jax import lax
from jax.experimental import pallas as pl
from jax.experimental.pallas import tpu as pltpu
from jax.sharding import PartitionSpec as P

exchange_fraction = 0.25
cell_ratio = 8.0
lines_own = 8
cube = 16
batch = 3
code_peak = 32700.0
MESH = pl.DeviceIdType.MESH
HBM_SPEC = pl.BlockSpec(memory_space=pltpu.HBM)
f32 = jnp.float32


def hartley(grid_len):
    rows_idx = np.arange(grid_len)
    angles = 2.0 * math.pi / grid_len * (rows_idx[:, None] * rows_idx[None, :] % grid_len)
    return ((np.cos(angles) + np.sin(angles)) / math.sqrt(grid_len)).astype(np.float32)


def split_const(values):
    high = values.astype(jnp.bfloat16)
    return high, (values - high.astype(np.float32)).astype(jnp.bfloat16)


def split(values):
    high = values.astype(jnp.bfloat16)
    low = (values - high.astype(f32)).astype(jnp.bfloat16)
    return high, low


def depth_turn(rows, depth_ref):
    width = rows.shape[1]
    high, low = split(rows)
    both = jnp.dot(jnp.concatenate([high, low], axis=1), depth_ref[...],
                   preferred_element_type=f32)
    return both[:, :width] + both[:, width:]


def left_turn(fields, left_ref):
    high, low = split(jnp.concatenate(fields, axis=1))
    return jnp.dot(left_ref[...], jnp.concatenate([high, low, high], axis=0),
                   preferred_element_type=f32)


def unit_of(level):
    return jnp.exp2(level * (1.0 / 64.0))


def encode(block):
    peak = jnp.max(jnp.abs(block), axis=0, keepdims=True)
    level = jnp.ceil(jnp.log2(jnp.maximum(peak, 1e-30) * (1.0 / code_peak)) * 64.0)
    return whole(block * unit_of(-level)), level


def whole(values):
    return jnp.round(values).astype(jnp.int32).astype(jnp.int16)


def plain(code):
    return code.astype(jnp.int32).astype(f32)


def decode(code, unit):
    return plain(code) * unit


def remote(src, dst, send_sem, recv_sem, device):
    return pltpu.make_async_remote_copy(src_ref=src, dst_ref=dst, send_sem=send_sem, recv_sem=recv_sem,
                                        device_id=device, device_id_type=MESH)


def flipped(index, bits):
    turned, bit = index, 1
    while bit <= bits:
        if bits & bit:
            turned = turned + bit - 2 * bit * (index // bit % 2)
        bit *= 2
    return turned


def spread_order(members, half):
    core = half
    plain = sorted((b for b in range(1, members) if not b & core), key=lambda b: (bin(b).count("1"), b))
    order, left = [], list(plain)
    while left:
        first = left.pop(0)
        order.append(first)
        rest = (max(members - 1 - core, 0)) ^ first
        if rest in left:
            left.remove(rest)
            order.append(rest)
    return order + [b | core for b in order] + [core] if members > core else order


def action_kernel(n_orb, n_slab, half, quota, chunks, grid_len, table_hbm, own_ref, depth_hbm,
                  turn_hbm, out_ref, unit_ref, *scratch):
    held = scratch[:chunks]
    (table_ref, depth_ref, turn_ref, tab_own, tables, tab_s, starts, ids, chosen, gain, kern, levels, fsend, frecv, units, work,
     turned, bsend, brecv, terms, parts, rsend, runit, rrecv, rrunit, overlap, packed,
     packed_in, merged, merged_in, coef, result, ysend, yunit,
     load_sem, out_sem, tab_sem, tab_send, tab_recv, own_sem, g_send, g_recv, stay_sem, f_send, f_recv, keep_sem, b_send,
     b_recv, r_send, r_recv, o_send, o_recv, p_send, p_recv, y_send, y_recv) = scratch[chunks:]
    me, me_slab = lax.axis_index("orb"), lax.axis_index("slab")
    group, part = me // half, me % half
    groups, members = n_orb // half, n_slab * half
    place = me_slab * half + part
    own_couples, _, width = own_ref.shape
    couples = n_orb * own_couples
    shared = half * own_couples
    capacity = table_ref.shape[1]
    lines = lines_own
    bands = grid_len // lines
    sets = members // bands
    slots = sets * quota
    runs = quota // batch
    own_planes = grid_len // members
    planes = own_planes // chunks
    rows = planes * grid_len
    tile = planes * lines
    slot_tiles = fsend.shape[2]
    stride = quota if quota <= 12 else batch

    def taker(which, band):
        return (band // half * sets + which) * half + band % half

    my_band = me_slab // sets * half + part

    near = spread_order(members, half)

    def line_to(step):
        return flipped(me, n_orb - step)

    def line_peer(step):
        return {"orb": line_to(step)}

    def member(step):
        to = flipped(place, near[step - 1])
        return to, {"orb": group * half + to % half, "slab": to // half}

    loads = [pltpu.make_async_copy(src, dst, load_sem.at[k]) for k, (src, dst) in enumerate(
        ((table_hbm, table_ref), (depth_hbm, depth_ref), (turn_hbm, turn_ref)))]

    barrier = pltpu.get_barrier_semaphore()
    for step in range(1, n_orb):
        pl.semaphore_signal(barrier, inc=1, device_id=line_peer(step), device_id_type=MESH)
    for slab_step in range(1, n_slab):
        for other in range(half):
            pl.semaphore_signal(
                barrier, inc=1, device_id={"orb": group * half + other,
                                           "slab": lax.rem(me_slab + slab_step, n_slab)},
                device_id_type=MESH)

    def plane_rows(which, chunk):
        return pl.ds(pl.multiple_of((which * chunks + chunk) * rows, rows), rows)

    def tab_copy(step):
        return remote(tab_own, tables.at[me], tab_send.at[step - 1], tab_recv.at[step - 1],
                      line_peer(step))

    def plane_row(which, plane):
        return pl.ds(pl.multiple_of((which * own_planes + plane) * grid_len, grid_len), grid_len)

    def gather_copy(chunk, step):
        to = line_to(step)
        return remote(own_ref.at[:, plane_rows(to % half, chunk)],
                      held[chunk].at[pl.ds(me * own_couples, own_couples)],
                      g_send.at[chunk, step - 1], g_recv.at[chunk, step - 1], line_peer(step))

    def own_copy(chunk):
        return pltpu.make_async_copy(own_ref.at[:, plane_rows(part, chunk)],
                                     held[chunk].at[pl.ds(me * own_couples, own_couples)],
                                     own_sem.at[chunk])

    def fwd_copy(chunk, step):
        to, device = member(step)
        return remote(fsend.at[chunk, to], frecv.at[chunk, place], f_send.at[chunk, step - 1],
                      f_recv.at[chunk, step - 1], device)

    def fwd_stay(chunk):
        return pltpu.make_async_copy(fsend.at[chunk, place], frecv.at[chunk, place], stay_sem.at[chunk])

    def back_copy(chunk, step, run=0):
        to, device = member(step)
        some, at = pl.ds(0, slot_tiles), runs - 1 + chunk
        if chunk == 0:
            some, at = pl.ds(run * batch, batch), run
            if isinstance(run, int) and run == runs - 1:
                some = pl.ds(run * batch, slot_tiles - run * batch)
        return remote(bsend.at[chunk, to, some], brecv.at[chunk, place, some], b_send.at[at, step - 1],
                      b_recv.at[at, step - 1], device)

    def back_parts(chunk, step):
        return [back_copy(chunk, step, run) for run in range(runs if chunk == 0 else 1)]

    def back_stay(chunk):
        return pltpu.make_async_copy(bsend.at[chunk, place], brecv.at[chunk, place], keep_sem.at[chunk])

    def sum_copies(plane, step):
        to = lax.rem(group + step, groups)
        theirs = pl.ds(to * shared, shared)
        device = {"orb": to * half + part}
        return (remote(rsend.at[plane, theirs], rrecv.at[plane, step - 1], r_send.at[0, plane, step - 1],
                       r_recv.at[0, plane, step - 1], device),
                remote(runit.at[plane, theirs], rrunit.at[plane, step - 1], r_send.at[1, plane, step - 1],
                       r_recv.at[1, plane, step - 1], device))

    def overlap_copy(step):
        to = lax.rem(group + step, groups)
        return remote(packed.at[to], packed_in.at[step - 1], o_send.at[step - 1], o_recv.at[step - 1],
                      {"orb": to * half + part})

    def merged_copy(step):
        return remote(merged, merged_in.at[step - 1], p_send.at[step - 1], p_recv.at[step - 1],
                      member(step)[1])

    def result_stay(plane):
        mine = pl.ds(part * own_couples, own_couples)
        return (pltpu.make_async_copy(ysend.at[plane, mine], out_ref.at[:, plane_row(part, plane)],
                                      out_sem.at[0, plane]),
                pltpu.make_async_copy(yunit.at[plane, mine], unit_ref.at[:, part * own_planes + plane],
                                      out_sem.at[1, plane]))

    def result_copies(plane, hop):
        to = flipped(part, hop)
        theirs, device = pl.ds(to * own_couples, own_couples), {"orb": group * half + to}
        return (remote(ysend.at[plane, theirs], out_ref.at[:, plane_row(part, plane)],
                       y_send.at[0, plane, hop - 1], y_recv.at[0, plane, hop - 1], device),
                remote(yunit.at[plane, theirs], unit_ref.at[:, part * own_planes + plane],
                       y_send.at[1, plane, hop - 1], y_recv.at[1, plane, hop - 1], device))

    for load in loads:
        load.start()
    tab_own[...] = jnp.full(tab_own.shape, -1, jnp.int32)
    loads[0].wait()
    tab_own[0:3, 0:capacity] = table_ref[...]
    kz = lax.broadcasted_iota(jnp.int32, (grid_len, width), 1) % grid_len
    fz = jnp.minimum(kz, grid_len - kz).astype(f32)
    ky = lax.broadcasted_iota(jnp.int32, (grid_len, width), 0)
    fy = jnp.minimum(ky, grid_len - ky).astype(f32)
    plane_sq = fy * fy + fz * fz
    deep = cell_ratio * cell_ratio
    gain[...] = 1.0 / jnp.where(plane_sq > 0, plane_sq, deep)
    fx = cell_ratio * fy
    scale_k = (2.0 * math.pi / grid_len) * (2.0 * math.pi / grid_len)
    for line in range(lines):
        at = my_band * lines + line
        fl = jnp.minimum(at, grid_len - at).astype(f32)
        plane = fl * fl + fz * fz
        full = fx * fx + plane
        level = jnp.where(plane > 0, plane, deep)
        kern[:, line * width:(line + 1) * width] = jnp.where(
            full > 0, (-exchange_fraction / scale_k) * level / jnp.where(full > 0, full, 1.0), 0.0)
    terms[2 * slots] = jnp.zeros(terms.shape[1:], f32)
    overlap[...] = jnp.zeros(overlap.shape, f32)
    levels[...] = jnp.zeros(levels.shape, f32)

    pl.semaphore_wait(barrier, n_orb - 1 + (n_slab - 1) * half)
    for step in range(1, n_orb):
        tab_copy(step).start()
    for chunk in range(chunks):
        for step in range(1, n_orb):
            gather_copy(chunk, step).start()
        own_copy(chunk).start()
    tables[me] = tab_own[...]

    for step in range(1, n_orb):
        tab_copy(step).wait_recv()
    to_scalars = pltpu.make_async_copy(tables, tab_s, tab_sem)
    to_scalars.start()
    to_scalars.wait()

    def count_block(block, total):
        starts[block] = total
        return lax.fori_loop(
            0, capacity, lambda k, sum_in: sum_in + (tab_s[block, 0, k] >= 0).astype(jnp.int32), total)

    live = lax.fori_loop(0, n_orb, count_block, jnp.int32(0))

    @pl.loop(0, slots)
    def _(slot):
        wanted = slot * groups + group
        used = wanted < live
        block = lax.fori_loop(
            1, n_orb, lambda b, sum_in: sum_in + (starts[b] <= wanted).astype(jnp.int32), jnp.int32(0))
        column = jnp.clip(wanted - starts[block], 0, capacity - 1)
        for k in range(3):
            ids[slot, k] = jnp.maximum(tab_s[block, k, column], 0)
        for k in range(2):
            ids[slot, 3 + k] = jnp.where(used, tab_s[block, k, column], -1)

    def pair_of(chunk, slot, span):
        left = held[chunk][ids[slot, 0], span].astype(f32)
        right = held[chunk][ids[slot, 1], span].astype(f32)
        crossed = ids[slot, 2] == 1
        return left, jnp.where(crossed, pltpu.roll(right, grid_len, 1), right), crossed

    def put_levels(ref, chunk, to):
        for k in range(slot_tiles - quota):
            ref[chunk, to, quota + k] = whole(levels[chunk, to, k * tile:(k + 1) * tile])

    def take_units(ref, chunk):
        for src in range(members):
            for k in range(slot_tiles - quota):
                units[chunk, src, k * tile:(k + 1) * tile] = unit_of(plain(ref[chunk, src, quota + k]))

    def advance(chunk):
        own_copy(chunk).wait()
        for step in range(1, n_orb):
            gather_copy(chunk, step).wait_recv()

        for which in range(sets):
            @pl.loop(0, quota, step=batch)
            def _(base):
                pairs = [pair_of(chunk, which * quota + base + k, slice(None)) for k in range(batch)]
                flat = depth_turn(jnp.concatenate([left * partner for left, partner, _ in pairs], axis=0),
                                  depth_ref)
                done = left_turn([flat[k * grid_len:(k + 1) * grid_len] for k in range(2 * batch)], turn_ref)
                for k in range(batch):
                    one = done[:, 2 * k * width:(2 * k + 1) * width] * gain[...]
                    two = done[:, (2 * k + 1) * width:(2 * k + 2) * width] * gain[...]
                    for band in range(bands):
                        to = taker(which, band)
                        span = slice(band * lines, (band + 1) * lines)
                        code, level = encode(jnp.concatenate([one[span], two[span]], axis=0))
                        fsend[chunk, to, base + k] = code
                        levels[chunk, to, pl.ds(base + k, 1)] = level

            for band in range(bands):
                put_levels(fsend, chunk, taker(which, band))
            for step in range(1, members):
                to = member(step)[0]

                @pl.when(to // half % sets == which)
                def _():
                    fwd_copy(chunk, step).start()

        fwd_stay(chunk).start()

    for load in loads[1:]:
        load.wait()
    for chunk in range(chunks):
        advance(chunk)

    @pl.loop(0, slots)
    def _(slot):
        @pl.loop(0, couples)
        def _(couple):
            chosen[couple, slot] = jnp.where(
                ids[slot, 3] == couple, 2 * slot, jnp.where(ids[slot, 4] == couple, 2 * slot + 1, 2 * slots))

    for chunk in range(chunks):
        fwd_stay(chunk).wait()
        for step in range(1, members):
            fwd_copy(chunk, step).wait_recv()

        take_units(frecv, chunk)

    @pl.loop(0, quota, step=batch)
    def _(base):
        for k in range(batch):
            for src in range(members):
                for chunk in range(chunks):
                    at = (src * chunks + chunk) * tile
                    work[k, at:at + tile] = decode(frecv[chunk, src, base + k],
                                                   units[chunk, src, pl.ds(base + k, 1)])
            done = left_turn([work[k, pl.ds(line, grid_len, stride=lines), :] for line in range(lines)],
                             turn_ref)
            done = done * kern[...]
            back = left_turn([done[:, line * width:(line + 1) * width] for line in range(lines)], turn_ref)
            for line in range(lines):
                turned[k, pl.ds(line, grid_len, stride=lines), :] = back[:, line * width:(line + 1) * width]
            for to in range(members):
                for chunk in range(chunks):
                    at = (to * chunks + chunk) * tile
                    code, level = encode(turned[k, at:at + tile])
                    bsend[chunk, to, base + k] = code
                    levels[chunk, to, pl.ds(base + k, 1)] = level

        @pl.when(base < quota - batch)
        def _():
            for step in range(1, members):
                back_copy(0, step, base // batch).start()

    for chunk in range(chunks):
        for to in range(members):
            put_levels(bsend, chunk, to)
        for step in range(1, members):
            back_copy(chunk, step, 0 if chunk else runs - 1).start()
        back_stay(chunk).start()

    def retreat(plane):
        chunk, sub = plane // planes, plane % planes
        if sub == 0:
            back_stay(chunk).wait()
            for step in range(1, members):
                for copy in back_parts(chunk, step):
                    copy.wait_recv()
            take_units(brecv, chunk)
        near_rows, span = slice(sub * lines, (sub + 1) * lines), slice(sub * grid_len, (sub + 1) * grid_len)

        for which in range(sets):
            @pl.loop(0, quota, step=stride)
            def _(base):
                fields = [
                    jnp.concatenate([decode(brecv[chunk, taker(which, band), base + k, near_rows],
                                            units[chunk, taker(which, band), pl.ds(base + k, 1)])
                                     for band in range(bands)], axis=0)
                    for k in range(stride)]
                done = left_turn(fields, turn_ref)
                potentials = depth_turn(jnp.concatenate(
                    [done[:, k * width:(k + 1) * width] for k in range(stride)], axis=0), depth_ref)
                for k in range(stride):
                    slot = which * quota + base + k
                    potential = potentials[k * grid_len:(k + 1) * grid_len]
                    left, partner, crossed = pair_of(chunk, slot, span)
                    terms[2 * slot] = potential * partner
                    second = potential * left
                    terms[2 * slot + 1] = jnp.where(crossed, pltpu.roll(second, grid_len, 1), second)

        @pl.loop(0, couples)
        def _(couple):
            total = terms[chosen[couple, 0]]
            for slot in range(1, slots):
                total = total + terms[chosen[couple, slot]]
            parts[plane, couple] = total
            code, level = encode(total)
            rsend[plane, couple] = code
            runit[plane, couple] = unit_of(level)
            across = pltpu.roll(total, grid_len, 1)
            at = couple % shared * couples
            for other in range(couples):
                basis = held[chunk][other, span].astype(f32)
                for kind, field in enumerate((total, across)):
                    row = pl.ds(at + kind * shared * couples + other, 1)
                    overlap[couple // shared, row] += jnp.sum(basis * field, axis=0, keepdims=True)

    for plane in range(own_planes - 1):
        retreat(plane)
        for step in range(1, groups):
            for copy in sum_copies(plane, step):
                copy.start()
    retreat(own_planes - 1)

    lane = lax.broadcasted_iota(jnp.int32, (8, width), 1)
    halves = ((lane // grid_len) == lax.broadcasted_iota(jnp.int32, (8, width), 0)).astype(jnp.bfloat16)

    def thirds(values):
        high = values.astype(jnp.bfloat16)
        rest = values - high.astype(f32)
        mid = rest.astype(jnp.bfloat16)
        return high, mid, (rest - mid.astype(f32)).astype(jnp.bfloat16)

    for which in range(groups):
        packed[which] = sum(lax.dot_general(halves, third, (((1,), (1,)), ((), ())),
                                            preferred_element_type=f32)
                            for third in thirds(overlap[which]))
    for step in range(1, groups):
        overlap_copy(step).start()
    for step in range(1, groups):
        for copy in sum_copies(own_planes - 1, step):
            copy.start()
    total = packed[group]
    for step in range(1, groups):
        overlap_copy(step).wait_recv()
        total = total + packed_in[step - 1]
    merged[...] = total
    for step in range(1, members):
        merged_copy(step).start()
    for step in range(1, members):
        merged_copy(step).wait_recv()
        total = total + merged_in[step - 1]
    total = total * (1.0 / (grid_len * grid_len * grid_len))
    coef[...] = sum(lax.dot_general(third, halves, (((0,), (0,)), ((), ())), preferred_element_type=f32)
                    for third in thirds(total))

    strip = grid_len // 2
    for plane in range(own_planes):
        chunk, first = plane // planes, plane % planes * grid_len
        for step in range(1, groups):
            for copy in sum_copies(plane, step):
                copy.wait_recv()

        @pl.loop(0, grid_len // strip)
        def _(at):
            here = pl.ds(pl.multiple_of(at * strip, strip), strip)
            there = pl.ds(pl.multiple_of(first + at * strip, strip), strip)
            kept = [jnp.zeros((strip, width), f32) for _ in range(2 * shared)]
            for couple in range(couples):
                basis = held[chunk][couple, there].astype(f32)
                for k in range(2 * shared):
                    row = k * couples + couple
                    kept[k] = kept[k] + coef[row:row + 1] * basis
            for k in range(shared):
                total = parts[plane, group * shared + k, here]
                for step in range(1, groups):
                    total = total + decode(rrecv[plane, step - 1, k, here], rrunit[plane, step - 1, k])
                result[k, here] = total - kept[k] - pltpu.roll(kept[shared + k], grid_len, 1)

        for k in range(shared):
            code, level = encode(result[k])
            ysend[plane, k] = code
            yunit[plane, k] = unit_of(level)
        for hop in range(1, half):
            for copy in result_copies(plane, hop):
                copy.start()
        for copy in result_stay(plane):
            copy.start()

    for plane in range(own_planes):
        for copy in result_stay(plane):
            copy.wait()
        for hop in range(1, half):
            for copy in result_copies(plane, hop):
                copy.wait()
        for step in range(1, groups):
            for copy in sum_copies(plane, step):
                copy.wait_send()
    for chunk in range(chunks):
        for step in range(1, members):
            fwd_copy(chunk, step).wait_send()
            for copy in back_parts(chunk, step):
                copy.wait_send()
        for step in range(1, n_orb):
            gather_copy(chunk, step).wait_send()
    for step in range(1, groups):
        overlap_copy(step).wait_send()
    for step in range(1, members):
        merged_copy(step).wait_send()
    for step in range(1, n_orb):
        tab_copy(step).wait_send()


def local(orbitals, pair_table, n_orb, n_slab):
    own_couples, slab_len, grid_len, width = orbitals.shape
    capacity = pair_table.shape[0]
    half = max(1, cube // n_slab)
    members = n_slab * half
    groups = n_orb // half
    bands = grid_len // lines_own
    sets = members // bands
    live_total = sum(capacity * (k + 1) // n_orb for k in range(n_orb))
    quota = -(-live_total // (groups * sets * batch)) * batch
    slots = sets * quota
    couples, shared = n_orb * own_couples, half * own_couples
    planes = grid_len // members
    chunks = planes // 2
    rows, tile = 2 * grid_len, 2 * lines_own
    level_tiles = -(-quota // tile)
    overlap_rows = -(-2 * shared * couples // 128) * 128
    tab_lanes = -(-capacity // 128) * 128

    mat = hartley(grid_len)
    mat_high, mat_low = split_const(mat)
    turn_mat = jnp.asarray(np.concatenate([mat_high, mat_high, mat_low], axis=1))
    deep_high, deep_low = split_const(np.kron(np.eye(2, dtype=np.float32), mat))
    depth_mat = jnp.asarray(np.block([[deep_high, deep_low], [deep_high, np.zeros_like(deep_low)]]))

    dma, vmem, smem = pltpu.SemaphoreType.DMA, pltpu.VMEM, pltpu.SMEM
    i32, i16 = jnp.int32, jnp.int16
    bf16 = orbitals.dtype
    coded = vmem((chunks, members, quota + level_tiles, tile, width), i16)
    per_slot = vmem((chunks, members, level_tiles * tile, width), f32)
    lines_sem = dma((chunks, n_orb - 1))
    cross_sem = dma((chunks, members - 1))
    back_sem = dma((quota // batch + chunks - 1, members - 1))
    steps = max(groups - 1, 1)
    sum_sem = dma((2, planes, steps))
    hops = max(half - 1, 1)
    code, unit = pl.pallas_call(
        functools.partial(action_kernel, n_orb, n_slab, half, quota, chunks, grid_len),
        out_shape=(jax.ShapeDtypeStruct((own_couples, slab_len * grid_len, width), i16),
                   jax.ShapeDtypeStruct((own_couples, slab_len, 1, width), f32)),
        in_specs=[HBM_SPEC] * 4,
        out_specs=(HBM_SPEC, HBM_SPEC),
        scratch_shapes=[vmem((couples, rows, width), orbitals.dtype)] * chunks + [
            vmem((3, capacity), i32), vmem(depth_mat.shape, bf16), vmem(turn_mat.shape, bf16),
            vmem((8, tab_lanes), i32), vmem((n_orb, 8, tab_lanes), i32), smem((n_orb, 8, tab_lanes), i32),
            smem((n_orb,), i32), smem((slots, 5), i32), smem((couples, slots), i32),
            vmem((grid_len, width), f32), vmem((grid_len, lines_own * width), f32),
            per_slot, coded, coded, per_slot,
            vmem((batch, lines_own * grid_len, width), f32), vmem((batch, lines_own * grid_len, width), f32),
            coded, coded,
            vmem((2 * slots + 1, grid_len, width), f32),
            vmem((planes, couples, grid_len, width), f32),
            vmem((planes, couples, grid_len, width), i16), vmem((planes, couples, 1, width), f32),
            vmem((planes, steps, shared, grid_len, width), i16), vmem((planes, steps, shared, 1, width), f32),
            vmem((groups, overlap_rows, width), f32), vmem((groups, 8, overlap_rows), f32),
            vmem((steps, 8, overlap_rows), f32), vmem((8, overlap_rows), f32),
            vmem((members - 1, 8, overlap_rows), f32), vmem((overlap_rows, width), f32),
            vmem((shared, grid_len, width), f32),
            vmem((planes, shared, grid_len, width), i16), vmem((planes, shared, 1, width), f32),
            dma((3,)), dma((2, planes)), dma, dma((n_orb - 1,)), dma((n_orb - 1,)), dma((chunks,)), lines_sem, lines_sem,
            dma((chunks,)), cross_sem, cross_sem, dma((chunks,)), back_sem, back_sem,
            sum_sem, sum_sem, dma((steps,)), dma((steps,)), dma((members - 1,)), dma((members - 1,)),
            dma((2, planes, hops)), dma((2, planes, hops)),
        ],
        compiler_params=pltpu.CompilerParams(collective_id=0, has_side_effects=True,
                                             vmem_limit_bytes=56 << 20),
    )(pair_table.T, orbitals.reshape(own_couples, slab_len * grid_len, width), depth_mat, turn_mat)
    return code.reshape(orbitals.shape).astype(f32) * unit


def solution(mesh):
    placed = (P("orb", "slab", None, None), P("orb", None))
    return jax.shard_map(
        functools.partial(local, n_orb=mesh.shape["orb"], n_slab=mesh.shape["slab"]),
        mesh=mesh, in_specs=placed, out_specs=P("orb", "slab", None, None), check_vma=False
    )
```

time: 79.1 us -> 73.7 us (0.932)
  Pallas kernels: 76.2 us -> 71.7 us
    pallas_call x1, Pallas kernels: 76.2 us -> 71.7 us  [local(): pl.pallas_call(functools.partial(action_kernel, n_orb, n_slab, half, quot...]
where the time goes in v5:
time: 73.7 us; the launch traced here: 73.6 us
  Pallas kernels  71.7 us (97%)
  other arithmetic  1.84 us (2%)
    pallas_call x1, Pallas kernels, local(): pl.pallas_call(functools.partial(action_kernel, n_orb, n_slab, half, quot...  71.7 us
    mul x1, other arithmetic, local(): return code.reshape(orbitals.shape).astype(f32) * unit  1.84 us

profile of v5, /device:TPU:0, one launch (start us, length us, event | category | flops | bytes accessed | tf_op | source)
XLA Modules:
  0.0 73.6 jit_solution(8925504129538056148)
XLA Ops:
  0.0 71.7 %shard_map.46 = (s16[1,1024,128]{2,1,0:T(8,128)(2,1)}, f32[1,16,1,128]{3,2,1,0:T(1,128)}) custom-call(s32[3,8]{1,0:T(4,128)} %bitcast.8, bf16[1,1024,128]{2,1,0:T(8,128)(2,1)} %bitcast.6, bf16[256,256]{1,0:T(8,128)(2,1)} %constant.5.clone.depth_hbm, bf16[64,192]{1,0:T(8,128)(2,1)} %constant.4.clone.turn_hbm), custom_call_target="tpu_custom_call" | custom-call | tf_op jit(solution)/shard_map/pallas_call | solution.py:578
  71.7 1.8 %convert_multiply_fusion = f32[1,16,64,128]{3,2,1,0:T(8,128)} fusion(s16[1,16,64,128]{3,2,1,0:T(8,128)(2,1)} %bitcast.5, f32[16,128]{1,0:T(8,128)} %bitcast.7), kind=kLoop, calls=%fused_computation | loop fusion | flops 262144 | bytes 794624 | tf_op jit(solution)/shard_map/mul | solution.py:609

commit v6 on v5

--- a/solution.py
+++ b/solution.py
@@ -104,10 +104,10 @@
 def action_kernel(n_orb, n_slab, half, quota, chunks, grid_len, table_hbm, own_ref, depth_hbm,
                   turn_hbm, out_ref, unit_ref, *scratch):
     held = scratch[:chunks]
-    (table_ref, depth_ref, turn_ref, tab_own, tables, tab_s, starts, ids, chosen, gain, kern, levels, fsend, frecv, units, work,
+    (table_ref, depth_ref, turn_ref, tab_own, tables, tab_s, starts, ids, chosen, gain, kern, levels, fsend, frecv, funit, funit_in, units, work,
      turned, bsend, brecv, terms, parts, rsend, runit, rrecv, rrunit, overlap, packed,
      packed_in, merged, merged_in, coef, result, ysend, yunit,
-     load_sem, out_sem, tab_sem, tab_send, tab_recv, own_sem, g_send, g_recv, stay_sem, f_send, f_recv, keep_sem, b_send,
+     load_sem, out_sem, tab_sem, tab_send, tab_recv, own_sem, g_send, g_recv, stay_sem, f_send, f_recv, s_send, s_recv, keep_sem, b_send,
      b_recv, r_send, r_recv, o_send, o_recv, p_send, p_recv, y_send, y_recv) = scratch[chunks:]
     me, me_slab = lax.axis_index("orb"), lax.axis_index("slab")
     group, part = me // half, me % half
@@ -127,7 +127,6 @@
     rows = planes * grid_len
     tile = planes * lines
     slot_tiles = fsend.shape[2]
-    stride = quota if quota <= 12 else batch
 
     def taker(which, band):
         return (band // half * sets + which) * half + band % half
@@ -163,8 +162,11 @@
         return pl.ds(pl.multiple_of((which * chunks + chunk) * rows, rows), rows)
 
     def tab_copy(step):
-        return remote(tab_own, tables.at[me], tab_send.at[step - 1], tab_recv.at[step - 1],
-                      line_peer(step))
+        return remote(tab_own, tables.at[me], tab_send, tab_recv, line_peer(step))
+
+    def tab_all():
+        every = tables.at[pl.ds(0, n_orb - 1)]
+        return remote(every, every, tab_send, tab_recv, line_peer(1))
 
     def plane_row(which, plane):
         return pl.ds(pl.multiple_of((which * own_planes + plane) * grid_len, grid_len), grid_len)
@@ -173,33 +175,77 @@
         to = line_to(step)
         return remote(own_ref.at[:, plane_rows(to % half, chunk)],
                       held[chunk].at[pl.ds(me * own_couples, own_couples)],
-                      g_send.at[chunk, step - 1], g_recv.at[chunk, step - 1], line_peer(step))
+                      g_send.at[chunk], g_recv.at[chunk], line_peer(step))
+
+    def gather_all(chunk):
+        every = held[chunk].at[pl.ds(0, couples - own_couples)]
+        return remote(every, every, g_send.at[chunk], g_recv.at[chunk], line_peer(1))
 
     def own_copy(chunk):
         return pltpu.make_async_copy(own_ref.at[:, plane_rows(part, chunk)],
                                      held[chunk].at[pl.ds(me * own_couples, own_couples)],
                                      own_sem.at[chunk])
 
+    last = chunks - 1
+
     def fwd_copy(chunk, step):
         to, device = member(step)
-        return remote(fsend.at[chunk, to], frecv.at[chunk, place], f_send.at[chunk, step - 1],
-                      f_recv.at[chunk, step - 1], device)
+        return remote(fsend.at[chunk, to], frecv.at[chunk, place], f_send.at[chunk], f_recv.at[chunk], device)
+
+    others = pl.ds(0, members - 1)
+
+    def fwd_all(chunk):
+        return remote(fsend.at[chunk, others], frecv.at[chunk, others], f_send.at[chunk], f_recv.at[chunk],
+                      member(1)[1])
 
     def fwd_stay(chunk):
         return pltpu.make_async_copy(fsend.at[chunk, place], frecv.at[chunk, place], stay_sem.at[chunk])
 
-    def back_copy(chunk, step, run=0):
+    def fwd_run(step, run):
         to, device = member(step)
-        some, at = pl.ds(0, slot_tiles), runs - 1 + chunk
-        if chunk == 0:
-            some, at = pl.ds(run * batch, batch), run
-            if isinstance(run, int) and run == runs - 1:
+        some = pl.ds(run * batch, batch)
+        at = last + run
+        return (remote(fsend.at[last, to, some], frecv.at[last, place, some], f_send.at[at], f_recv.at[at],
+                       device),
+                remote(funit.at[to, run], funit_in.at[place, run], s_send.at[run], s_recv.at[run], device))
+
+    def fwd_run_all(run):
+        some = pl.ds(run * batch, batch)
+        at = last + run
+        return (remote(fsend.at[last, others, some], frecv.at[last, others, some], f_send.at[at],
+                       f_recv.at[at], member(1)[1]),
+                remote(funit.at[others, run], funit_in.at[others, run], s_send.at[run], s_recv.at[run],
+                       member(1)[1]))
+
+    def fwd_stay_run(run):
+        some = pl.ds(run * batch, batch)
+        return (pltpu.make_async_copy(fsend.at[last, place, some], frecv.at[last, place, some],
+                                      stay_sem.at[last + run]),
+                pltpu.make_async_copy(funit.at[place, run], funit_in.at[place, run],
+                                      stay_sem.at[last + runs + run]))
+
+    def slot_at(chunk, slot):
+        return slot + (slot_tiles - quota if chunk == last else 0)
+
+    def back_run(chunk, run):
+        some, at = pl.ds(slot_at(chunk, run * batch), batch), chunk * runs + run
+        if isinstance(run, int):
+            if chunk == last and run == 0:
+                some = pl.ds(0, slot_tiles - quota + batch)
+            elif chunk < last and run == runs - 1:
                 some = pl.ds(run * batch, slot_tiles - run * batch)
-        return remote(bsend.at[chunk, to, some], brecv.at[chunk, place, some], b_send.at[at, step - 1],
-                      b_recv.at[at, step - 1], device)
-
-    def back_parts(chunk, step):
-        return [back_copy(chunk, step, run) for run in range(runs if chunk == 0 else 1)]
+        return some, at
+
+    def back_copy(chunk, step, run):
+        to, device = member(step)
+        some, at = back_run(chunk, run)
+        return remote(bsend.at[chunk, to, some], brecv.at[chunk, place, some], b_send.at[at], b_recv.at[at],
+                      device)
+
+    def back_all(chunk, run):
+        some, at = back_run(chunk, run)
+        return remote(bsend.at[chunk, others, some], brecv.at[chunk, others, some], b_send.at[at],
+                      b_recv.at[at], member(1)[1])
 
     def back_stay(chunk):
         return pltpu.make_async_copy(bsend.at[chunk, place], brecv.at[chunk, place], keep_sem.at[chunk])
@@ -208,19 +254,29 @@
         to = lax.rem(group + step, groups)
         theirs = pl.ds(to * shared, shared)
         device = {"orb": to * half + part}
-        return (remote(rsend.at[plane, theirs], rrecv.at[plane, step - 1], r_send.at[0, plane, step - 1],
-                       r_recv.at[0, plane, step - 1], device),
-                remote(runit.at[plane, theirs], rrunit.at[plane, step - 1], r_send.at[1, plane, step - 1],
-                       r_recv.at[1, plane, step - 1], device))
+        return (remote(rsend.at[plane, theirs], rrecv.at[plane, step - 1], r_send.at[0, plane],
+                       r_recv.at[0, plane], device),
+                remote(runit.at[plane, theirs], rrunit.at[plane, step - 1], r_send.at[1, plane],
+                       r_recv.at[1, plane], device))
+
+    def sum_all(plane):
+        device = {"orb": lax.rem(group + 1, groups) * half + part}
+        return [remote(ref.at[plane], ref.at[plane], r_send.at[k, plane], r_recv.at[k, plane], device)
+                for k, ref in enumerate((rrecv, rrunit))]
 
     def overlap_copy(step):
         to = lax.rem(group + step, groups)
-        return remote(packed.at[to], packed_in.at[step - 1], o_send.at[step - 1], o_recv.at[step - 1],
+        return remote(packed.at[to], packed_in.at[step - 1], o_send, o_recv,
                       {"orb": to * half + part})
 
+    def overlap_all():
+        return remote(packed_in, packed_in, o_send, o_recv, {"orb": lax.rem(group + 1, groups) * half + part})
+
     def merged_copy(step):
-        return remote(merged, merged_in.at[step - 1], p_send.at[step - 1], p_recv.at[step - 1],
-                      member(step)[1])
+        return remote(merged, merged_in.at[step - 1], p_send, p_recv, member(step)[1])
+
+    def merged_all():
+        return remote(merged_in, merged_in, p_send, p_recv, member(1)[1])
 
     def result_stay(plane):
         mine = pl.ds(part * own_couples, own_couples)
@@ -233,9 +289,15 @@
         to = flipped(part, hop)
         theirs, device = pl.ds(to * own_couples, own_couples), {"orb": group * half + to}
         return (remote(ysend.at[plane, theirs], out_ref.at[:, plane_row(part, plane)],
-                       y_send.at[0, plane, hop - 1], y_recv.at[0, plane, hop - 1], device),
+                       y_send.at[0], y_recv.at[0], device),
                 remote(yunit.at[plane, theirs], unit_ref.at[:, part * own_planes + plane],
-                       y_send.at[1, plane, hop - 1], y_recv.at[1, plane, hop - 1], device))
+                       y_send.at[1], y_recv.at[1], device))
+
+    def result_all():
+        theirs = pl.ds(0, shared - own_couples)
+        device = {"orb": group * half + flipped(part, 1)}
+        return [remote(ref.at[:, theirs], ref.at[:, theirs], y_send.at[k], y_recv.at[k], device)
+                for k, ref in enumerate((ysend, yunit))]
 
     for load in loads:
         load.start()
@@ -272,8 +334,7 @@
         own_copy(chunk).start()
     tables[me] = tab_own[...]
 
-    for step in range(1, n_orb):
-        tab_copy(step).wait_recv()
+    tab_all().wait_recv()
     to_scalars = pltpu.make_async_copy(tables, tab_s, tab_sem)
     to_scalars.start()
     to_scalars.wait()
@@ -303,47 +364,65 @@
         crossed = ids[slot, 2] == 1
         return left, jnp.where(crossed, pltpu.roll(right, grid_len, 1), right), crossed
 
-    def put_levels(ref, chunk, to):
+    def put_levels(ref, chunk, to, first):
         for k in range(slot_tiles - quota):
-            ref[chunk, to, quota + k] = whole(levels[chunk, to, k * tile:(k + 1) * tile])
-
-    def take_units(ref, chunk):
+            ref[chunk, to, first + k] = whole(levels[chunk, to, k * tile:(k + 1) * tile])
+
+    def take_units(ref, chunk, first):
         for src in range(members):
             for k in range(slot_tiles - quota):
-                units[chunk, src, k * tile:(k + 1) * tile] = unit_of(plain(ref[chunk, src, quota + k]))
+                units[chunk, src, k * tile:(k + 1) * tile] = unit_of(plain(ref[chunk, src, first + k]))
 
     def advance(chunk):
         own_copy(chunk).wait()
-        for step in range(1, n_orb):
-            gather_copy(chunk, step).wait_recv()
-
-        for which in range(sets):
-            @pl.loop(0, quota, step=batch)
-            def _(base):
-                pairs = [pair_of(chunk, which * quota + base + k, slice(None)) for k in range(batch)]
-                flat = depth_turn(jnp.concatenate([left * partner for left, partner, _ in pairs], axis=0),
-                                  depth_ref)
-                done = left_turn([flat[k * grid_len:(k + 1) * grid_len] for k in range(2 * batch)], turn_ref)
-                for k in range(batch):
-                    one = done[:, 2 * k * width:(2 * k + 1) * width] * gain[...]
-                    two = done[:, (2 * k + 1) * width:(2 * k + 2) * width] * gain[...]
-                    for band in range(bands):
-                        to = taker(which, band)
-                        span = slice(band * lines, (band + 1) * lines)
-                        code, level = encode(jnp.concatenate([one[span], two[span]], axis=0))
-                        fsend[chunk, to, base + k] = code
-                        levels[chunk, to, pl.ds(base + k, 1)] = level
-
-            for band in range(bands):
-                put_levels(fsend, chunk, taker(which, band))
-            for step in range(1, members):
-                to = member(step)[0]
-
-                @pl.when(to // half % sets == which)
-                def _():
-                    fwd_copy(chunk, step).start()
-
-        fwd_stay(chunk).start()
+        gather_all(chunk).wait_recv()
+
+        def densities(which, base, keep):
+            pairs = [pair_of(chunk, which * quota + base + k, slice(None)) for k in range(batch)]
+            flat = depth_turn(jnp.concatenate([left * partner for left, partner, _ in pairs], axis=0),
+                              depth_ref)
+            done = left_turn([flat[k * grid_len:(k + 1) * grid_len] for k in range(2 * batch)], turn_ref)
+            for k in range(batch):
+                one = done[:, 2 * k * width:(2 * k + 1) * width] * gain[...]
+                two = done[:, (2 * k + 1) * width:(2 * k + 2) * width] * gain[...]
+                for band in range(bands):
+                    to = taker(which, band)
+                    span = slice(band * lines, (band + 1) * lines)
+                    code, level = encode(jnp.concatenate([one[span], two[span]], axis=0))
+                    fsend[chunk, to, base + k] = code
+                    keep(to, base, k, level)
+
+        def keep_level(to, base, k, level):
+            levels[chunk, to, pl.ds(base + k, 1)] = level
+
+        def keep_unit(to, base, k, level):
+            funit[to, base // batch, k] = unit_of(level)
+
+        if chunk < last:
+            for which in range(sets):
+                @pl.loop(0, quota, step=batch)
+                def _(base):
+                    densities(which, base, keep_level)
+
+                for band in range(bands):
+                    put_levels(fsend, chunk, taker(which, band), quota)
+                for step in range(1, members):
+                    to = member(step)[0]
+
+                    @pl.when(to // half % sets == which)
+                    def _():
+                        fwd_copy(chunk, step).start()
+
+            fwd_stay(chunk).start()
+        else:
+            for run in range(runs):
+                for which in range(sets):
+                    densities(which, run * batch, keep_unit)
+                for step in range(1, members):
+                    for copy in fwd_run(step, run):
+                        copy.start()
+                for copy in fwd_stay_run(run):
+                    copy.start()
 
     for load in loads[1:]:
         load.wait()
@@ -357,21 +436,24 @@
             chosen[couple, slot] = jnp.where(
                 ids[slot, 3] == couple, 2 * slot, jnp.where(ids[slot, 4] == couple, 2 * slot + 1, 2 * slots))
 
-    for chunk in range(chunks):
+    for chunk in range(last):
         fwd_stay(chunk).wait()
-        for step in range(1, members):
-            fwd_copy(chunk, step).wait_recv()
-
-        take_units(frecv, chunk)
-
-    @pl.loop(0, quota, step=batch)
-    def _(base):
+        fwd_all(chunk).wait_recv()
+        take_units(frecv, chunk, quota)
+
+    for run in range(runs):
+        base = run * batch
+        for copy in fwd_stay_run(run):
+            copy.wait()
+        for copy in fwd_run_all(run):
+            copy.wait_recv()
         for k in range(batch):
             for src in range(members):
                 for chunk in range(chunks):
                     at = (src * chunks + chunk) * tile
-                    work[k, at:at + tile] = decode(frecv[chunk, src, base + k],
-                                                   units[chunk, src, pl.ds(base + k, 1)])
+                    unit = (units[chunk, src, pl.ds(base + k, 1)] if chunk < last
+                            else funit_in[src, run, k])
+                    work[k, at:at + tile] = decode(frecv[chunk, src, base + k], unit)
             done = left_turn([work[k, pl.ds(line, grid_len, stride=lines), :] for line in range(lines)],
                              turn_ref)
             done = done * kern[...]
@@ -382,55 +464,71 @@
                 for chunk in range(chunks):
                     at = (to * chunks + chunk) * tile
                     code, level = encode(turned[k, at:at + tile])
-                    bsend[chunk, to, base + k] = code
+                    bsend[chunk, to, slot_at(chunk, base + k)] = code
                     levels[chunk, to, pl.ds(base + k, 1)] = level
 
-        @pl.when(base < quota - batch)
-        def _():
-            for step in range(1, members):
-                back_copy(0, step, base // batch).start()
+        if run < runs - 1:
+            for chunk in range(last):
+                for step in range(1, members):
+                    back_copy(chunk, step, run).start()
 
     for chunk in range(chunks):
         for to in range(members):
-            put_levels(bsend, chunk, to)
-        for step in range(1, members):
-            back_copy(chunk, step, 0 if chunk else runs - 1).start()
+            put_levels(bsend, chunk, to, 0 if chunk == last else quota)
+        for run in range(0 if chunk == last else runs - 1, runs):
+            for step in range(1, members):
+                back_copy(chunk, step, run).start()
         back_stay(chunk).start()
 
-    def retreat(plane):
-        chunk, sub = plane // planes, plane % planes
-        if sub == 0:
-            back_stay(chunk).wait()
-            for step in range(1, members):
-                for copy in back_parts(chunk, step):
-                    copy.wait_recv()
-            take_units(brecv, chunk)
-        near_rows, span = slice(sub * lines, (sub + 1) * lines), slice(sub * grid_len, (sub + 1) * grid_len)
-
-        for which in range(sets):
-            @pl.loop(0, quota, step=stride)
+    def retreat(chunk):
+        def potentials_of(base):
+            slots_at = [(which, base + k) for which in range(sets) for k in range(batch)]
+            fields = []
+            for which, slot in slots_at:
+                blocks = [decode(brecv[chunk, taker(which, band), slot_at(chunk, slot)],
+                                 units[chunk, taker(which, band), pl.ds(slot, 1)])
+                          for band in range(bands)]
+                for k in range(planes):
+                    fields.append(jnp.concatenate([block[k * lines:(k + 1) * lines] for block in blocks],
+                                                  axis=0))
+            done = left_turn(fields, turn_ref)
+            deep = depth_turn(jnp.concatenate(
+                [done[:, k * width:(k + 1) * width] for k in range(len(fields))], axis=0), depth_ref)
+            for k, (which, place_in) in enumerate(slots_at):
+                slot = which * quota + place_in
+                potential = deep[k * rows:(k + 1) * rows]
+                left, partner, crossed = pair_of(chunk, slot, slice(None))
+                terms[2 * slot] = potential * partner
+                second = potential * left
+                terms[2 * slot + 1] = jnp.where(crossed, pltpu.roll(second, grid_len, 1), second)
+
+        back_stay(chunk).wait()
+        if chunk < last:
+            for run in range(runs):
+                back_all(chunk, run).wait_recv()
+            take_units(brecv, chunk, quota)
+
+            @pl.loop(0, quota, step=batch)
             def _(base):
-                fields = [
-                    jnp.concatenate([decode(brecv[chunk, taker(which, band), base + k, near_rows],
-                                            units[chunk, taker(which, band), pl.ds(base + k, 1)])
-                                     for band in range(bands)], axis=0)
-                    for k in range(stride)]
-                done = left_turn(fields, turn_ref)
-                potentials = depth_turn(jnp.concatenate(
-                    [done[:, k * width:(k + 1) * width] for k in range(stride)], axis=0), depth_ref)
-                for k in range(stride):
-                    slot = which * quota + base + k
-                    potential = potentials[k * grid_len:(k + 1) * grid_len]
-                    left, partner, crossed = pair_of(chunk, slot, span)
-                    terms[2 * slot] = potential * partner
-                    second = potential * left
-                    terms[2 * slot + 1] = jnp.where(crossed, pltpu.roll(second, grid_len, 1), second)
+                potentials_of(base)
+        else:
+            back_all(chunk, 0).wait_recv()
+            take_units(brecv, chunk, 0)
+            potentials_of(0)
+
+            for run in range(1, runs):
+                back_all(chunk, run).wait_recv()
+                potentials_of(run * batch)
+
+    def finish(plane):
+        chunk = plane // planes
+        span = slice(plane % planes * grid_len, (plane % planes + 1) * grid_len)
 
         @pl.loop(0, couples)
         def _(couple):
-            total = terms[chosen[couple, 0]]
+            total = terms[chosen[couple, 0], span]
             for slot in range(1, slots):
-                total = total + terms[chosen[couple, slot]]
+                total = total + terms[chosen[couple, slot], span]
             parts[plane, couple] = total
             code, level = encode(total)
             rsend[plane, couple] = code
@@ -443,12 +541,14 @@
                     row = pl.ds(at + kind * shared * couples + other, 1)
                     overlap[couple // shared, row] += jnp.sum(basis * field, axis=0, keepdims=True)
 
-    for plane in range(own_planes - 1):
-        retreat(plane)
-        for step in range(1, groups):
-            for copy in sum_copies(plane, step):
-                copy.start()
-    retreat(own_planes - 1)
+    for plane in range(own_planes):
+        if plane % planes == 0:
+            retreat(plane // planes)
+        finish(plane)
+        if plane < own_planes - 1:
+            for step in range(1, groups):
+                for copy in sum_copies(plane, step):
+                    copy.start()
 
     lane = lax.broadcasted_iota(jnp.int32, (8, width), 1)
     halves = ((lane // grid_len) == lax.broadcasted_iota(jnp.int32, (8, width), 0)).astype(jnp.bfloat16)
@@ -469,14 +569,14 @@
         for copy in sum_copies(own_planes - 1, step):
             copy.start()
     total = packed[group]
+    overlap_all().wait_recv()
     for step in range(1, groups):
-        overlap_copy(step).wait_recv()
         total = total + packed_in[step - 1]
     merged[...] = total
     for step in range(1, members):
         merged_copy(step).start()
+    merged_all().wait_recv()
     for step in range(1, members):
-        merged_copy(step).wait_recv()
         total = total + merged_in[step - 1]
     total = total * (1.0 / (grid_len * grid_len * grid_len))
     coef[...] = sum(lax.dot_general(third, halves, (((0,), (0,)), ((), ())), preferred_element_type=f32)
@@ -485,9 +585,8 @@
     strip = grid_len // 2
     for plane in range(own_planes):
         chunk, first = plane // planes, plane % planes * grid_len
-        for step in range(1, groups):
-            for copy in sum_copies(plane, step):
-                copy.wait_recv()
+        for copy in sum_all(plane):
+            copy.wait_recv()
 
         @pl.loop(0, grid_len // strip)
         def _(at):
@@ -518,25 +617,23 @@
     for plane in range(own_planes):
         for copy in result_stay(plane):
             copy.wait()
-        for hop in range(1, half):
-            for copy in result_copies(plane, hop):
-                copy.wait()
-        for step in range(1, groups):
-            for copy in sum_copies(plane, step):
-                copy.wait_send()
+        for copy in sum_all(plane):
+            copy.wait_send()
+    if half > 1:
+        for copy in result_all():
+            copy.wait()
+    for run in range(runs):
+        for copy in fwd_run_all(run):
+            copy.wait_send()
     for chunk in range(chunks):
-        for step in range(1, members):
-            fwd_copy(chunk, step).wait_send()
-            for copy in back_parts(chunk, step):
-                copy.wait_send()
-        for step in range(1, n_orb):
-            gather_copy(chunk, step).wait_send()
-    for step in range(1, groups):
-        overlap_copy(step).wait_send()
-    for step in range(1, members):
-        merged_copy(step).wait_send()
-    for step in range(1, n_orb):
-        tab_copy(step).wait_send()
+        if chunk < last:
+            fwd_all(chunk).wait_send()
+        for run in range(runs):
+            back_all(chunk, run).wait_send()
+        gather_all(chunk).wait_send()
+    overlap_all().wait_send()
+    merged_all().wait_send()
+    tab_all().wait_send()
 
 
 def local(orbitals, pair_table, n_orb, n_slab):
@@ -568,13 +665,10 @@
     i32, i16 = jnp.int32, jnp.int16
     bf16 = orbitals.dtype
     coded = vmem((chunks, members, quota + level_tiles, tile, width), i16)
+    runs = quota // batch
+    small_units = vmem((members, runs, batch, 1, width), f32)
     per_slot = vmem((chunks, members, level_tiles * tile, width), f32)
-    lines_sem = dma((chunks, n_orb - 1))
-    cross_sem = dma((chunks, members - 1))
-    back_sem = dma((quota // batch + chunks - 1, members - 1))
     steps = max(groups - 1, 1)
-    sum_sem = dma((2, planes, steps))
-    hops = max(half - 1, 1)
     code, unit = pl.pallas_call(
         functools.partial(action_kernel, n_orb, n_slab, half, quota, chunks, grid_len),
         out_shape=(jax.ShapeDtypeStruct((own_couples, slab_len * grid_len, width), i16),
@@ -586,10 +680,10 @@
             vmem((8, tab_lanes), i32), vmem((n_orb, 8, tab_lanes), i32), smem((n_orb, 8, tab_lanes), i32),
             smem((n_orb,), i32), smem((slots, 5), i32), smem((couples, slots), i32),
             vmem((grid_len, width), f32), vmem((grid_len, lines_own * width), f32),
-            per_slot, coded, coded, per_slot,
+            per_slot, coded, coded, small_units, small_units, per_slot,
             vmem((batch, lines_own * grid_len, width), f32), vmem((batch, lines_own * grid_len, width), f32),
             coded, coded,
-            vmem((2 * slots + 1, grid_len, width), f32),
+            vmem((2 * slots + 1, rows, width), f32),
             vmem((planes, couples, grid_len, width), f32),
             vmem((planes, couples, grid_len, width), i16), vmem((planes, couples, 1, width), f32),
             vmem((planes, steps, shared, grid_len, width), i16), vmem((planes, steps, shared, 1, width), f32),
@@ -598,10 +692,10 @@
             vmem((members - 1, 8, overlap_rows), f32), vmem((overlap_rows, width), f32),
             vmem((shared, grid_len, width), f32),
             vmem((planes, shared, grid_len, width), i16), vmem((planes, shared, 1, width), f32),
-            dma((3,)), dma((2, planes)), dma, dma((n_orb - 1,)), dma((n_orb - 1,)), dma((chunks,)), lines_sem, lines_sem,
-            dma((chunks,)), cross_sem, cross_sem, dma((chunks,)), back_sem, back_sem,
-            sum_sem, sum_sem, dma((steps,)), dma((steps,)), dma((members - 1,)), dma((members - 1,)),
-            dma((2, planes, hops)), dma((2, planes, hops)),
+            dma((3,)), dma((2, planes)), dma, dma, dma, dma((chunks,)), dma((chunks,)), dma((chunks,)),
+            dma((chunks - 1 + 2 * runs,)), dma((chunks - 1 + runs,)), dma((chunks - 1 + runs,)),
+            dma((runs,)), dma((runs,)), dma((chunks,)), dma((runs * chunks,)), dma((runs * chunks,)),
+            dma((2, planes)), dma((2, planes)), dma, dma, dma, dma, dma((2,)), dma((2,)),
         ],
         compiler_params=pltpu.CompilerParams(collective_id=0, has_side_effects=True,
                                              vmem_limit_bytes=56 << 20),

time: 73.7 us -> 70.4 us (0.955)
  Pallas kernels: 71.7 us -> 68.4 us
    pallas_call x1, Pallas kernels: 71.7 us -> 68.4 us  [local(): pl.pallas_call(functools.partial(action_kernel, n_orb, n_slab, half, quot...]
where the time goes in v6:
time: 70.4 us; the launch traced here: 70.3 us
  Pallas kernels  68.4 us (97%)
  other arithmetic  1.84 us (3%)
    pallas_call x1, Pallas kernels, local(): pl.pallas_call(functools.partial(action_kernel, n_orb, n_slab, half, quot...  68.4 us
    mul x1, other arithmetic, local(): return code.reshape(orbitals.shape).astype(f32) * unit  1.84 us

profile of v6, /device:TPU:0, one launch (start us, length us, event | category | flops | bytes accessed | tf_op | source)
XLA Modules:
  0.0 70.3 jit_solution(17597439392644425721)
XLA Ops:
  0.0 68.4 %shard_map.46 = (s16[1,1024,128]{2,1,0:T(8,128)(2,1)}, f32[1,16,1,128]{3,2,1,0:T(1,128)}) custom-call(s32[3,8]{1,0:T(4,128)} %bitcast.8, bf16[1,1024,128]{2,1,0:T(8,128)(2,1)} %bitcast.6, bf16[256,256]{1,0:T(8,128)(2,1)} %constant.5.clone.depth_hbm, bf16[64,192]{1,0:T(8,128)(2,1)} %constant.4.clone.turn_hbm), custom_call_target="tpu_custom_call" | custom-call | tf_op jit(solution)/shard_map/pallas_call | solution.py:672
  68.4 1.8 %convert_multiply_fusion = f32[1,16,64,128]{3,2,1,0:T(8,128)} fusion(s16[1,16,64,128]{3,2,1,0:T(8,128)(2,1)} %bitcast.5, f32[16,128]{1,0:T(8,128)} %bitcast.7), kind=kLoop, calls=%fused_computation | loop fusion | flops 262144 | bytes 794624 | tf_op jit(solution)/shard_map/mul | solution.py:703

commit v7 on v6

--- a/solution.py
+++ b/solution.py
@@ -533,6 +533,19 @@
             code, level = encode(total)
             rsend[plane, couple] = code
             runit[plane, couple] = unit_of(level)
+
+    def send_sums(plane):
+        for step in range(1, groups):
+            for copy in sum_copies(plane, step):
+                copy.start()
+
+    def project(plane):
+        chunk = plane // planes
+        span = slice(plane % planes * grid_len, (plane % planes + 1) * grid_len)
+
+        @pl.loop(0, couples)
+        def _(couple):
+            total = parts[plane, couple]
             across = pltpu.roll(total, grid_len, 1)
             at = couple % shared * couples
             for other in range(couples):
@@ -546,9 +559,11 @@
             retreat(plane // planes)
         finish(plane)
         if plane < own_planes - 1:
-            for step in range(1, groups):
-                for copy in sum_copies(plane, step):
-                    copy.start()
+            send_sums(plane)
+        if plane < own_planes - planes:
+            project(plane)
+    for plane in range(own_planes - planes, own_planes):
+        project(plane)
 
     lane = lax.broadcasted_iota(jnp.int32, (8, width), 1)
     halves = ((lane // grid_len) == lax.broadcasted_iota(jnp.int32, (8, width), 0)).astype(jnp.bfloat16)
@@ -565,9 +580,6 @@
                             for third in thirds(overlap[which]))
     for step in range(1, groups):
         overlap_copy(step).start()
-    for step in range(1, groups):
-        for copy in sum_copies(own_planes - 1, step):
-            copy.start()
     total = packed[group]
     overlap_all().wait_recv()
     for step in range(1, groups):
@@ -575,6 +587,9 @@
     merged[...] = total
     for step in range(1, members):
         merged_copy(step).start()
+    for step in range(1, groups):
+        for copy in sum_copies(own_planes - 1, step):
+            copy.start()
     merged_all().wait_recv()
     for step in range(1, members):
         total = total + merged_in[step - 1]

time: 70.4 us -> 69.3 us (0.984)
  Pallas kernels: 68.4 us -> 67.3 us
    pallas_call x1, Pallas kernels: 68.4 us -> 67.3 us  [local(): pl.pallas_call(functools.partial(action_kernel, n_orb, n_slab, half, quot...]
where the time goes in v7:
time: 69.3 us; the launch traced here: 69.1 us
  Pallas kernels  67.3 us (97%)
  other arithmetic  1.84 us (3%)
    pallas_call x1, Pallas kernels, local(): pl.pallas_call(functools.partial(action_kernel, n_orb, n_slab, half, quot...  67.3 us
    mul x1, other arithmetic, local(): return code.reshape(orbitals.shape).astype(f32) * unit  1.84 us

profile of v7, /device:TPU:0, one launch (start us, length us, event | category | flops | bytes accessed | tf_op | source)
XLA Modules:
  0.0 69.1 jit_solution(5673315653841092742)
XLA Ops:
  0.0 67.3 %shard_map.46 = (s16[1,1024,128]{2,1,0:T(8,128)(2,1)}, f32[1,16,1,128]{3,2,1,0:T(1,128)}) custom-call(s32[3,8]{1,0:T(4,128)} %bitcast.8, bf16[1,1024,128]{2,1,0:T(8,128)(2,1)} %bitcast.6, bf16[256,256]{1,0:T(8,128)(2,1)} %constant.5.clone.depth_hbm, bf16[64,192]{1,0:T(8,128)(2,1)} %constant.4.clone.turn_hbm), custom_call_target="tpu_custom_call" | custom-call | tf_op jit(solution)/shard_map/pallas_call | solution.py:687
  67.3 1.8 %convert_multiply_fusion = f32[1,16,64,128]{3,2,1,0:T(8,128)} fusion(s16[1,16,64,128]{3,2,1,0:T(8,128)(2,1)} %bitcast.5, f32[16,128]{1,0:T(8,128)} %bitcast.7), kind=kLoop, calls=%fused_computation | loop fusion | flops 262144 | bytes 794624 | tf_op jit(solution)/shard_map/mul | solution.py:718

commit v8 on v7

--- a/solution.py
+++ b/solution.py
@@ -57,7 +57,7 @@
 
 def encode(block):
     peak = jnp.max(jnp.abs(block), axis=0, keepdims=True)
-    level = jnp.ceil(jnp.log2(jnp.maximum(peak, 1e-30) * (1.0 / code_peak)) * 64.0)
+    level = jnp.ceil(jnp.log2(jnp.maximum(peak, 1e-33) * (1.0 / code_peak)) * 64.0)
     return whole(block * unit_of(-level)), level
 
 

time: 69.3 us -> 69.3 us (level)
  no operation moved by 1% of the time
where the time goes in v8:
time: 69.3 us; the launch traced here: 69.1 us
  Pallas kernels  67.3 us (97%)
  other arithmetic  1.84 us (3%)
    pallas_call x1, Pallas kernels, local(): pl.pallas_call(functools.partial(action_kernel, n_orb, n_slab, half, quot...  67.3 us
    mul x1, other arithmetic, local(): return code.reshape(orbitals.shape).astype(f32) * unit  1.84 us

profile of v8, /device:TPU:0, one launch (start us, length us, event | category | flops | bytes accessed | tf_op | source)
XLA Modules:
  0.0 69.1 jit_solution(15783977441468267922)
XLA Ops:
  0.0 67.3 %shard_map.46 = (s16[1,1024,128]{2,1,0:T(8,128)(2,1)}, f32[1,16,1,128]{3,2,1,0:T(1,128)}) custom-call(s32[3,8]{1,0:T(4,128)} %bitcast.8, bf16[1,1024,128]{2,1,0:T(8,128)(2,1)} %bitcast.6, bf16[256,256]{1,0:T(8,128)(2,1)} %constant.5.clone.depth_hbm, bf16[64,192]{1,0:T(8,128)(2,1)} %constant.4.clone.turn_hbm), custom_call_target="tpu_custom_call" | custom-call | tf_op jit(solution)/shard_map/pallas_call | solution.py:687
  67.3 1.8 %convert_multiply_fusion = f32[1,16,64,128]{3,2,1,0:T(8,128)} fusion(s16[1,16,64,128]{3,2,1,0:T(8,128)(2,1)} %bitcast.5, f32[16,128]{1,0:T(8,128)} %bitcast.7), kind=kLoop, calls=%fused_computation | loop fusion | flops 262144 | bytes 794624 | tf_op jit(solution)/shard_map/mul | solution.py:718
